TPU v7x, 256 devices: a whole 4x4x8 slice. The times are simulated.
256 devices in a mesh: seq: 64 (over x, z_lo, y, core), tensor: 4 (over z_hi).
Axes of the slice: x: 4, y: 4, z: 8 (z_hi: 4, z_lo: 2; z = z_hi * 2 + z_lo), core: 2. Of those that a mesh axis runs over, the one named last changes fastest.
Arguments:
- hidden: bfloat16 [8192, 2048], P('seq'), may hold values from -6 to 6
- attn_gain: float32 [2048], replicated, may hold values from 0.1 to 1.9
- w_query: bfloat16 [2048, 1536], P(None, 'tensor'), may hold values from -0.125 to 0.125
- w_latent_down: bfloat16 [2048, 576], replicated, may hold values from -0.125 to 0.125
- kv_gain: float32 [512], replicated, may hold values from 0.1 to 1.9
- w_key_up: bfloat16 [512, 1024], P(None, 'tensor'), may hold values from -5 to 5
- w_value_up: bfloat16 [512, 1024], P(None, 'tensor'), may hold values from -2 to 2
- w_out: bfloat16 [1024, 2048], P('tensor'), may hold values from -0.1875 to 0.1875
- ffn_gain: float32 [2048], replicated, may hold values from 0.1 to 1.9
- w_gate_exp: bfloat16 [64, 2048, 1408], P('seq', None, 'tensor'), may hold values from -0.125 to 0.125
- w_up_exp: bfloat16 [64, 2048, 1408], P('seq', None, 'tensor'), may hold values from -0.125 to 0.125
- w_down_exp: bfloat16 [64, 1408, 2048], P('seq', 'tensor'), may hold values from -0.15625 to 0.15625
- page_pool: bfloat16 [64, 128, 576], P('seq'), may hold values from -6 to 6
- page_table: int32 [4, 16], replicated, may hold values from 0 to 63, as said below
- request_group: int32 [16], replicated, may hold values from 0 to 3, as said below
- suffix_lengths: int32 [16], replicated, may hold values from 1 to 2048, 8192 in all
- token_order: int32 [8192], replicated, may hold values from 0 to 8191, each once
- expert_ids: int32 [8192, 6], P('seq'), may hold values from 0 to 63, all different within a row; in each aligned block of 128 rows (0 to 127, 128 to 255, ...) at most 14 rows name the same one
- expert_gates: float32 [8192, 6], P('seq'), may hold values from 0.2 to 0.8
Outputs:
- hidden_out: bfloat16 [8192, 2048], P('seq', 'tensor')
- latent_cache: bfloat16 [8192, 576], P('seq', 'tensor')
Inputs may be any that keep to these rules, and one draw needn't show every extreme that they name: `page_table`: each page id appears exactly once; row g lists the pages of group g's prefix. `request_group`: each group has exactly 4 requests. `suffix_lengths`: the lengths sum to 8192; the longest is exactly 2048. `token_order`: each concatenated position appears once. `expert_ids`: each row names 6 different experts; among the rows of one index of seq no expert is named more than 14 times, and on some indices one is named exactly 14 times.
All inputs are finite; a program needn't handle non-finite values.
Results may differ from a plain program's by a relative error of at most 0.017.
Values may be sent and summed in bfloat16 or wider, within the bound.
No kernel may reach another device: no remote copies, remote signals or barrier semaphores. Data moves between devices by JAX's collectives and lax.ppermute only.
A program may use at most 128 MiB of HBM per device.

v0:
```python
import functools

import jax
import jax.numpy as jnp
import numpy as np
from jax import lax
from jax.experimental import pallas as pl
from jax.experimental.pallas import tpu as pltpu
from jax.sharding import PartitionSpec as P

NOPE = 128
ROPE = 64
VDIM = 128
LATENT = 512
KEY = LATENT + ROPE
SLOTS = 16
EPSILON = 1e-06
ROPE_BASE = 50000.0
MASKED = -1e30

NX, NZ, NY, NC = 4, 2, 4, 2
BF = jnp.bfloat16
F32 = jnp.float32
VM = pltpu.MemorySpace.VMEM
SM = pltpu.MemorySpace.SMEM


def seq_id(x, z, y, c):
    return (((x % NX) * NZ + z % NZ) * NY + y % NY) * NC + c % NC


def seq_perm(dx, dz, dy, dc):
    pairs = []
    for x in range(NX):
        for z in range(NZ):
            for y in range(NY):
                for c in range(NC):
                    pairs.append((seq_id(x + dx, z + dz, y + dy, c + dc), seq_id(x, z, y, c)))
    return pairs


def tensor_from(d, n):
    return [((t + d) % n, t) for t in range(n)]


def zy_groups():
    return [
        [seq_id(x, z, y, c) for z in range(NZ) for y in range(NY)]
        for x in range(NX)
        for c in range(NC)
    ]


def my_place():
    s = lax.axis_index("seq")
    c = lax.rem(s, NC)
    y = lax.rem(lax.div(s, NC), NY)
    z = lax.rem(lax.div(s, NC * NY), NZ)
    x = lax.div(s, NC * NY * NZ)
    return x, z, y, c


def dot(a, b, dims=(((1,), (0,)), ((), ()))):
    return lax.dot_general(a, b, dims, preferred_element_type=F32)


def token_rows(tok, lengths, group):
    tok = tok.astype(F32)
    start = jnp.zeros_like(tok)
    grp = jnp.zeros_like(tok)
    end = jnp.int32(0)
    for r in range(lengths.shape[0]):
        begin = end
        end = end + lengths[r]
        ef = end.astype(F32)
        bf = begin.astype(F32)
        past = tok >= ef
        start = jnp.where(past, ef, start)
        if group is not None:
            inside = jnp.logical_and(tok >= bf, tok < ef)
            grp = jnp.where(inside, group[r].astype(F32), grp)
    return tok, start, grp


def to_columns(rows, n):
    which = lax.broadcasted_iota(jnp.int32, (n, n), 0)
    out = jnp.zeros((n, n), F32)
    for i, row in enumerate(rows):
        out = jnp.where(which == i, jnp.broadcast_to(row, (n, n)), out)
    return out.T


def project_kernel(prefix, lengths, tok_ref, freq_ref, hid_ref, gain_ref, wq_ref, wl_ref, kvg_ref, q_ref, lat_ref):
    n = hid_ref.shape[0]
    s = lax.axis_index("seq")
    tok, start, _ = token_rows(tok_ref[pl.ds(s, 1), :], lengths, None)
    position = to_columns([tok - start + float(prefix)], n)[:, 0:1]
    angles = position * freq_ref[...]
    lane = lax.broadcasted_iota(jnp.int32, (n, 128), 1)
    first = lax.rem(lane, ROPE) < ROPE // 2
    cos = jnp.cos(angles)
    sin = jnp.where(first, -jnp.sin(angles), jnp.sin(angles))

    def rotate(v):
        partner = jnp.where(first, pltpu.roll(v, 128 - ROPE // 2, 1), pltpu.roll(v, ROPE // 2, 1))
        return v * cos + partner * sin

    hid = hid_ref[...].astype(F32)
    scale = lax.rsqrt(jnp.mean(hid * hid, axis=-1, keepdims=True) + EPSILON)
    normed = (hid * scale * gain_ref[...]).astype(BF)
    query = dot(normed, wq_ref[...]).astype(BF)
    width = NOPE + ROPE
    pe = jnp.concatenate([query[:, NOPE:width], query[:, width + NOPE : 2 * width]], axis=1)
    q_ref[:, 0:128] = query[:, 0:NOPE]
    q_ref[:, 128:256] = query[:, width : width + NOPE]
    q_ref[:, 256:384] = rotate(pe.astype(F32)).astype(BF)
    raw = dot(normed, wl_ref[...])
    lat = raw[:, :LATENT]
    lscale = lax.rsqrt(jnp.mean(lat * lat, axis=-1, keepdims=True) + EPSILON)
    lat_ref[:, :LATENT] = (lat * lscale * kvg_ref[...]).astype(BF)
    pe = raw[:, LATENT:]
    lat_ref[:, LATENT:] = rotate(jnp.concatenate([pe, pe], axis=1))[:, :ROPE].astype(BF)


def attend_kernel(
    place, lengths, group, table, tok_ref, q_ref, pa_ref, pb_ref, la_ref, lb_ref, ku_ref, vu_ref,
    out_ref, s_ref, qf_ref, owner,
):
    j = pl.program_id(0)
    n = q_ref.shape[1]
    x, z, y, c = place[0], place[1], place[2], place[3]

    @pl.when(j == 0)
    def _():
        for g in range(table.shape[0]):
            for i in range(table.shape[1]):
                owner[table[g, i]] = g

    me = seq_id(x, z + lax.div(j, NY), y + lax.rem(j, NY), c)
    tok, start, grp = token_rows(tok_ref[pl.ds(me, 1), :], lengths, group)
    cols = to_columns([tok, start, grp], n)
    two = jnp.concatenate([cols, cols], axis=0)
    pos_q, start_q, grp_q = two[:, 0:1], two[:, 1:2], two[:, 2:3]

    for h in range(2):
        up = ku_ref[:, h * NOPE : (h + 1) * NOPE]
        nope = q_ref[0, :, h * NOPE : (h + 1) * NOPE]
        qf_ref[h * n : (h + 1) * n, :LATENT] = dot(nope, up, (((1,), (1,)), ((), ()))).astype(BF)
        qf_ref[h * n : (h + 1) * n, LATENT:] = q_ref[0, :, 2 * NOPE + h * ROPE : 2 * NOPE + (h + 1) * ROPE]
    qf = qf_ref[...]
    keys = (pa_ref, pb_ref, la_ref, lb_ref)
    high = jnp.full((2 * n, 1), MASKED, F32)
    for b, k_ref in enumerate(keys):
        sc = dot(qf, k_ref[...], (((1,), (1,)), ((), ())))
        for i in range(NX):
            holder = seq_id(x + i, z, y, c + b % 2)
            part = sc[:, i * n : (i + 1) * n]
            if b < 2:
                bias = jnp.where(grp_q == owner[holder].astype(F32), 0.0, MASKED)
                part = part + bias
            else:
                pos_k = tok_ref[pl.ds(holder, 1), :].astype(F32)
                seen = jnp.logical_and(pos_k >= start_q, pos_k <= pos_q)
                part = jnp.where(seen, part, MASKED)
            s_ref[:, (b * NX + i) * n : (b * NX + i + 1) * n] = part
            high = jnp.maximum(high, jnp.max(part, axis=-1, keepdims=True))
    scale = (NOPE + ROPE) ** (-0.5)
    log2e = 1.4426950408889634
    top = jnp.where(high > 0.5 * MASKED, high, 0.0)
    den = jnp.zeros((2 * n, 1), F32)
    acc = jnp.zeros((2 * n, LATENT), F32)
    width = NX * n
    for b, k_ref in enumerate(keys):
        w = jnp.exp2((s_ref[:, b * width : (b + 1) * width] - top) * (scale * log2e))
        den = den + jnp.sum(w, axis=-1, keepdims=True)
        acc = acc + dot(w.astype(BF), k_ref[:, :LATENT])
    some = den > 0.0
    att = (acc / jnp.where(some, den, 1.0)).astype(BF)
    lse = jnp.where(some, top * scale + jnp.log(jnp.where(some, den, 1.0)), MASKED)
    hi = lse.astype(BF).astype(F32)
    mid = (lse - hi).astype(BF).astype(F32)
    low = lse - hi - mid
    lane = lax.broadcasted_iota(jnp.int32, (n, 128), 1)
    stat = jnp.zeros((n, 128), F32)
    for h in range(2):
        rows = slice(h * n, (h + 1) * n)
        out_ref[0, :, h * VDIM : (h + 1) * VDIM] = dot(
            att[rows], vu_ref[:, h * VDIM : (h + 1) * VDIM]
        ).astype(BF)
        for i, term in enumerate((hi, mid, low)):
            stat = jnp.where(lane == 3 * h + i, term[rows], stat)
    out_ref[0, :, 2 * VDIM :] = stat.astype(BF)


def project_out_kernel(got_ref, wo_ref, *outs):
    t = lax.axis_index("tensor")
    m = got_ref.shape[0]
    vals = []
    for h in range(2):
        lse = []
        for i in range(m):
            st = got_ref[i, :, 2 * VDIM :].astype(F32)
            lse.append(st[:, 3 * h : 3 * h + 1] + st[:, 3 * h + 1 : 3 * h + 2] + st[:, 3 * h + 2 : 3 * h + 3])
        top = functools.reduce(jnp.maximum, lse)
        den = jnp.zeros_like(top)
        acc = jnp.zeros((got_ref.shape[1], VDIM), F32)
        for i in range(m):
            w = jnp.exp(lse[i] - top)
            den = den + w
            acc = acc + w * got_ref[i, :, h * VDIM : (h + 1) * VDIM].astype(F32)
        vals.append((acc / den).astype(BF))
    vals = jnp.concatenate(vals, axis=1)
    q = outs[0].shape[1]
    for j, out in enumerate(outs):
        col = pl.multiple_of(lax.rem(t + j, len(outs)) * q, q)
        out[...] = dot(vals, wo_ref[:, pl.ds(col, q)]).astype(BF)


def mix_kernel(hid_ref, a_ref, b_ref, c_ref, d_ref, out_ref):
    t = lax.axis_index("tensor")
    q = out_ref.shape[1]
    col = pl.multiple_of(t * q, q)
    total = a_ref[...].astype(F32) + b_ref[...].astype(F32) + c_ref[...].astype(F32) + d_ref[...].astype(F32)
    out_ref[...] = (hid_ref[:, pl.ds(col, q)].astype(F32) + total).astype(BF)


def finish_kernel(mix_ref, a_ref, b_ref, c_ref, d_ref, out_ref):
    total = a_ref[...].astype(F32) + b_ref[...].astype(F32) + c_ref[...].astype(F32) + d_ref[...].astype(F32)
    out_ref[...] = (mix_ref[...].astype(F32) + total).astype(BF)


def slots_kernel(ids_ref, gates_ref, oh_ref, hi_ref, lo_ref):
    experts = oh_ref.shape[0] // SLOTS
    n = oh_ref.shape[1]
    which = lax.broadcasted_iota(jnp.int32, (experts, n), 0)
    named = jnp.zeros((experts, n), F32)
    gate = jnp.zeros((experts, n), F32)
    for k in range(ids_ref.shape[0]):
        hit = which == ids_ref[k : k + 1, :]
        named = jnp.where(hit, 1.0, named)
        gate = jnp.where(hit, gates_ref[k : k + 1, :], gate)
    before = lax.broadcasted_iota(jnp.int32, (n, n), 0) < lax.broadcasted_iota(jnp.int32, (n, n), 1)
    count = dot(named.astype(BF), jnp.where(before, 1.0, 0.0).astype(BF))
    slot = jnp.where(named > 0.0, count, -1.0)
    ghi = gate.astype(BF).astype(F32)
    glo = gate - ghi
    level = lax.broadcasted_iota(jnp.int32, (SLOTS, n), 0).astype(F32)
    for e in range(experts):
        hit = slot[e : e + 1, :] == level
        rows = slice(e * SLOTS, (e + 1) * SLOTS)
        oh_ref[rows, :] = jnp.where(hit, 1.0, 0.0).astype(BF)
        hi_ref[rows, :] = jnp.where(hit, ghi[e : e + 1, :], 0.0).astype(BF)
        lo_ref[rows, :] = jnp.where(hit, glo[e : e + 1, :], 0.0).astype(BF)


def dispatch_kernel(a_ref, b_ref, c_ref, d_ref, gain_ref, oh_ref, out_ref, in_ref):
    parts = (a_ref, b_ref, c_ref, d_ref)
    q = a_ref.shape[1]
    t = lax.axis_index("tensor")

    @pl.when(pl.program_id(0) == 0)
    def _():
        sq = jnp.zeros((a_ref.shape[0], 1), F32)
        for p in parts:
            v = p[...].astype(F32)
            sq = sq + jnp.sum(v * v, axis=-1, keepdims=True)
        scale = lax.rsqrt(sq / (q * len(parts)) + EPSILON)
        for j, p in enumerate(parts):
            col = pl.multiple_of(lax.rem(t + j, len(parts)) * q, q)
            in_ref[:, pl.ds(col, q)] = (p[...].astype(F32) * scale * gain_ref[:, pl.ds(col, q)]).astype(BF)

    out_ref[...] = dot(oh_ref[...], in_ref[...]).astype(BF)


def expert_kernel(x_ref, wg_ref, wu_ref, wd_ref, out_ref):
    x = x_ref[...]
    gate = dot(x, wg_ref[...])
    up = dot(x, wu_ref[...])
    act = (gate / (1.0 + jnp.exp(-gate)) * up).astype(BF)
    out_ref[...] = dot(act, wd_ref[...]).astype(BF)


def combine_kernel(rows_ref, hi_ref, lo_ref, *outs):
    t = lax.axis_index("tensor")
    q = outs[0].shape[1]
    tn = (((0,), (0,)), ((), ()))
    for j, out in enumerate(outs):
        col = pl.multiple_of(lax.rem(t + j, len(outs)) * q, q)
        rows = rows_ref[:, pl.ds(col, q)]
        out[...] = (dot(hi_ref[...], rows, tn) + dot(lo_ref[...], rows, tn)).astype(BF)


def whole(n):
    return [pl.BlockSpec(memory_space=VM)] * n


def local(
    hidden, attn_gain, w_query, w_latent_down, kv_gain, w_key_up, w_value_up, w_out, ffn_gain,
    w_gate_exp, w_up_exp, w_down_exp, page_pool, page_table, request_group, suffix_lengths,
    token_order, expert_ids, expert_gates,
):
    seq_count = lax.axis_size("seq")
    tensor_count = lax.axis_size("tensor")
    tensor_index = lax.axis_index("tensor")
    n, d = hidden.shape
    quarter = d // tensor_count
    prefix = page_table.shape[1] * page_pool.shape[1]
    tok = token_order.reshape(seq_count, n)
    place = jnp.stack(my_place()).astype(jnp.int32)
    params = pltpu.CompilerParams(vmem_limit_bytes=56 << 20)

    def spread(piece):
        got = [lax.ppermute(piece, "seq", seq_perm(i, 0, 0, 0)) for i in range(1, NX)]
        own = jnp.concatenate([piece] + got, axis=0)
        return own, lax.ppermute(own, "seq", seq_perm(0, 0, 0, 1))

    pages_a, pages_b = spread(page_pool[0])

    freq = ROPE_BASE ** (-2.0 * np.arange(ROPE // 2, dtype=np.float64) / ROPE)
    freq = jnp.asarray(np.tile(freq, 4)[None, :], F32)
    query, latent_cache = pl.pallas_call(
        functools.partial(project_kernel, prefix),
        out_shape=(
            jax.ShapeDtypeStruct((n, w_query.shape[1]), BF),
            jax.ShapeDtypeStruct((n, KEY), BF),
        ),
        in_specs=[pl.BlockSpec(memory_space=SM)] + whole(7),
        out_specs=tuple(whole(2)),
        compiler_params=params,
        name="project",
    )(suffix_lengths, tok, freq, hidden, attn_gain.reshape(1, d), w_query, w_latent_down, kv_gain.reshape(1, LATENT))

    lat_a, lat_b = spread(latent_cache)
    peers = [(i // NY, i % NY) for i in range(NZ * NY)]
    queries = jnp.stack(
        [query if i == 0 else lax.ppermute(query, "seq", seq_perm(0, dz, dy, 0)) for i, (dz, dy) in enumerate(peers)]
    )

    oh, ghi, glo = pl.pallas_call(
        slots_kernel,
        out_shape=(jax.ShapeDtypeStruct((seq_count * SLOTS, n), BF),) * 3,
        in_specs=whole(2),
        out_specs=tuple(whole(3)),
        compiler_params=params,
        name="slots",
    )(expert_ids.T, expert_gates.T)

    m = len(peers)
    keys = NX * n

    def place_of(j, place, *_):
        return (lax.rem(place[1] + lax.div(j, NY), NZ) * NY + lax.rem(place[2] + lax.rem(j, NY), NY), 0, 0)

    def fixed(shape):
        return pl.BlockSpec(shape, lambda j, *_: (0,) * len(shape))

    partial = pl.pallas_call(
        attend_kernel,
        out_shape=jax.ShapeDtypeStruct((m, n, 3 * VDIM), BF),
        grid_spec=pltpu.PrefetchScalarGridSpec(
            num_scalar_prefetch=4,
            grid=(m,),
            in_specs=[
                fixed(tok.shape),
                pl.BlockSpec((1, n, query.shape[1]), lambda j, *_: (j, 0, 0)),
                fixed((keys, KEY)),
                fixed((keys, KEY)),
                fixed((keys, KEY)),
                fixed((keys, KEY)),
                fixed(w_key_up.shape),
                fixed(w_value_up.shape),
            ],
            out_specs=pl.BlockSpec((1, n, 3 * VDIM), place_of),
            scratch_shapes=[
                pltpu.VMEM((2 * n, 4 * keys), F32),
                pltpu.VMEM((2 * n, KEY), BF),
                pltpu.SMEM((seq_count,), jnp.int32),
            ],
        ),
        compiler_params=params,
        name="attend",
    )(place, suffix_lengths, request_group, page_table, tok, queries, pages_a, pages_b, lat_a, lat_b, w_key_up, w_value_up)

    got = lax.all_to_all(partial, "seq", 0, 0, tiled=True, axis_index_groups=zy_groups())

    piece = jax.ShapeDtypeStruct((n, quarter), BF)

    def exchange(parts):
        return [parts[0]] + [
            lax.ppermute(parts[j], "tensor", tensor_from(-j, tensor_count)) for j in range(1, tensor_count)
        ]

    heads = pl.pallas_call(
        project_out_kernel,
        out_shape=(piece,) * tensor_count,
        in_specs=whole(2),
        out_specs=tuple(whole(tensor_count)),
        compiler_params=params,
        name="project_out",
    )(got, w_out)
    mixed = pl.pallas_call(
        mix_kernel, out_shape=piece, in_specs=whole(5), out_specs=whole(1)[0], compiler_params=params, name="mix"
    )(hidden, *exchange(heads))
    mixed_all = [mixed] + [
        lax.ppermute(mixed, "tensor", tensor_from(j, tensor_count)) for j in range(1, tensor_count)
    ]
    rows = seq_count * SLOTS
    block = rows // 4
    outbound = pl.pallas_call(
        dispatch_kernel,
        out_shape=jax.ShapeDtypeStruct((rows, d), BF),
        grid=(rows // block,),
        in_specs=[pl.BlockSpec((n, quarter), lambda i: (0, 0))] * 4
        + [pl.BlockSpec((1, d), lambda i: (0, 0)), pl.BlockSpec((block, n), lambda i: (i, 0))],
        out_specs=pl.BlockSpec((block, d), lambda i: (i, 0)),
        scratch_shapes=[pltpu.VMEM((n, d), BF)],
        compiler_params=params,
        name="dispatch",
    )(*mixed_all, ffn_gain.reshape(1, d), oh)
    arrived = lax.all_to_all(outbound.reshape(seq_count, SLOTS, d), "seq", 0, 0, tiled=True)
    hid = w_gate_exp.shape[2]
    results = pl.pallas_call(
        expert_kernel,
        out_shape=jax.ShapeDtypeStruct((rows, d), BF),
        grid=(rows // block,),
        in_specs=[
            pl.BlockSpec((block, d), lambda i: (i, 0)),
            pl.BlockSpec((d, hid), lambda i: (0, 0)),
            pl.BlockSpec((d, hid), lambda i: (0, 0)),
            pl.BlockSpec((hid, d), lambda i: (0, 0)),
        ],
        out_specs=pl.BlockSpec((block, d), lambda i: (i, 0)),
        compiler_params=params,
        name="expert",
    )(arrived.reshape(rows, d), w_gate_exp[0], w_up_exp[0], w_down_exp[0])
    back = lax.all_to_all(results.reshape(seq_count, SLOTS, d), "seq", 0, 0, tiled=True)
    sums = pl.pallas_call(
        combine_kernel,
        out_shape=(piece,) * tensor_count,
        in_specs=whole(3),
        out_specs=tuple(whole(tensor_count)),
        compiler_params=params,
        name="combine",
    )(back.reshape(rows, d), ghi, glo)
    hidden_out = pl.pallas_call(
        finish_kernel, out_shape=piece, in_specs=whole(5), out_specs=whole(1)[0], compiler_params=params, name="finish"
    )(mixed, *exchange(sums))
    width = KEY // tensor_count
    cache_part = lax.dynamic_slice_in_dim(latent_cache, tensor_index * width, width, 1)
    return (hidden_out, cache_part)


def solution(mesh):
    placed = (
        P("seq", None),
        P(),
        P(None, "tensor"),
        P(),
        P(),
        P(None, "tensor"),
        P(None, "tensor"),
        P("tensor", None),
        P(),
        P("seq", None, "tensor"),
        P("seq", None, "tensor"),
        P("seq", "tensor", None),
        P("seq", None, None),
        P(),
        P(),
        P(),
        P(),
        P("seq", None),
        P("seq", None),
    )
    return jax.shard_map(
        local,
        mesh=mesh,
        in_specs=placed,
        out_specs=(P("seq", "tensor"), P("seq", "tensor")),
        check_vma=False,
    )
```

profile of v0, /device:TPU:1, one launch (start us, length us, event | category | flops | bytes accessed | tf_op | source)
XLA Modules:
  0.0 303.8 jit_solution(12847425983992008841)
XLA Ops:
  0.6 1.1 copy.28
  1.7 2.1 collective-permute-start.9
  3.8 2.5 collective-permute-start.8
  6.2 1.2 collective-permute-start.7
  7.4 4.3 %copy.27.wl_ref = bf16[2048,576]{1,0:T(8,128)(2,1)} copy(bf16[2048,576]{0,1:T(8,128)(2,1)} %param.23) | data formatting | bytes 4718592 | tf_op args[3]
  11.7 4.3 %project.1 = (bf16[128,384]{1,0:T(8,128)(2,1)}, bf16[128,576]{1,0:T(8,128)(2,1)}) custom-call(s32[16]{0:T(128)} %lengths.3, s32[64,128]{1,0:T(8,128)} %bitcast.44, f32[1,128]{1,0:T(1,128)} %constant.36.clone.freq_ref, bf16[128,2048]{1,0:T(8,128)(2,1)} %hid_ref.3, f32[1,2048]{1,0:T(1,128)} %bitcast.46, bf16[2048,384]{1,0:T(8,128)(2,1)} %wq_ref.1, ...), custom_call_target="tpu_custom_call" | custom-call | tf_op jit(solution)/shard_map/project/pallas_call | solution.py:321
  16.0 2.7 collective-permute-start.6
  18.7 1.4 collective-permute-start
  20.1 0.9 bitcast_dynamic-update-slice_fusion.7
  21.0 0.9 constant_dynamic-update-slice_fusion.3
  22.0 0.6 pad_add_fusion.place
  22.5 2.7 collective-permute-start.1
  25.3 2.4 collective-permute-done.1
  27.7 1.4 collective-permute-start.2
  29.1 3.4 %collective-permute-done.2 = bf16[128,384]{1,0:T(8,128)(2,1)S(1)} collective-permute-done((bf16[128,384]{1,0:T(8,128)(2,1)}, bf16[128,384]{1,0:T(8,128)(2,1)S(1)}, u32[]{:S(2)}, u32[]{:S(2)}) %collective-permute-start.2) | collective-permute-done | bytes 98336 | tf_op jit(solution)/shard_map/ppermute | solution.py:336
  32.6 0.3 collective-permute-start.3
  32.9 3.6 %collective-permute-done.3 = bf16[128,384]{1,0:T(8,128)(2,1)S(1)} collective-permute-done((bf16[128,384]{1,0:T(8,128)(2,1)}, bf16[128,384]{1,0:T(8,128)(2,1)S(1)}, u32[]{:S(2)}, u32[]{:S(2)}) %collective-permute-start.3) | collective-permute-done | bytes 98336 | tf_op jit(solution)/shard_map/ppermute | solution.py:336
  36.6 1.8 collective-permute-start.5
  38.4 2.1 collective-permute-start.4
  40.5 2.1 collective-permute-start.12
  43.1 3.4 %collective-permute-done.12 = bf16[128,576]{1,0:T(8,128)(2,1)} collective-permute-done((bf16[128,576]{1,0:T(8,128)(2,1)}, bf16[128,576]{1,0:T(8,128)(2,1)}, u32[]{:S(2)}, u32[]{:S(2)}) %collective-permute-start.12) | collective-permute-done | bytes 147488 | tf_op jit(solution)/shard_map/ppermute | solution.py:313
  46.5 8.1 %collective-permute-start.10 = (bf16[512,576]{0,1:T(8,128)(2,1)S(1)}, bf16[512,576]{0,1:T(8,128)(2,1)S(1)}, u32[]{:S(2)}, u32[]{:S(2)}) collective-permute-start(bf16[512,576]{0,1:T(8,128)(2,1)S(1)} %copy.29), channel_id=1, source_target_pairs={{4,0},{0,4},{12,8},{8,12},{20,16},{16,20},{28,24},{24,28},{36,32},... | collective-permute-start | bytes 1769480 | tf_op jit(solution)/shard_map/ppermute | solution.py:315
  54.6 0.9 constant_dynamic-update-slice_fusion.1
  55.6 1.1 copy.30
  56.7 0.7 collective-permute-start.14
  57.4 0.9 bitcast_dynamic-update-slice_fusion.2
  58.3 0.9 bitcast_dynamic-update-slice_fusion.1
  59.3 1.1 copy.31.pb_ref
  60.4 2.1 copy.32.lb_ref
  62.5 21.5 %attend.1 = bf16[8,128,384]{2,1,0:T(8,128)(2,1)} custom-call(s32[4]{0:T(128)} %pad_add_fusion.place, s32[16]{0:T(128)} %lengths.3, s32[16]{0:T(128)} %group.1, s32[4,16]{1,0:T(4,128)} %table.1, s32[64,128]{1,0:T(8,128)} %bitcast.45, bf16[8,128,384]{2,1,0:T(8,128)(2,1)} %copy-done.4, bf16[512,576]{1,0:T(8,128)(2,1)} %copy-done, ...), custom_call_target="tpu_custom_call" | custom-call | tf_op jit(solution)/shard_map/attend/pallas_call | solution.py:357
  84.0 16.5 %all_to_all.15.got_ref = bf16[8,128,384]{2,1,0:T(8,128)(2,1)} all-to-all(bf16[8,128,384]{2,1,0:T(8,128)(2,1)} %attend.1), channel_id=1, replica_groups={{0,8,16,24,32,40,48,56},{4,12,20,28,36,44,52,60},{64,72,80,88,96,104,11..., dimensions={0} | all-to-all | bytes 1572864 | tf_op jit(solution)/shard_map/all_to_all | solution.py:384
  100.5 3.0 project_out.1
  103.5 2.9 collective-permute-start.15
  106.5 4.4 %collective-permute-start.16 = (bf16[128,512]{1,0:T(8,128)(2,1)}, bf16[128,512]{1,0:T(8,128)(2,1)S(1)}, u32[]{:S(2)}, u32[]{:S(2)}) collective-permute-start(bf16[128,512]{1,0:T(8,128)(2,1)} %get-tuple-element.19), channel_id=1, source_target_pairs={{2,0},{3,1},{0,2},{1,3},{6,4},{7,5},{4,6},{5,7},{10,8},{11,9},{8,1... | collective-permute-start | bytes 393224 | tf_op jit(solution)/shard_map/ppermute | solution.py:390
  110.8 2.4 collective-permute-start.17
  113.2 5.8 %collective-permute-done.16.c_ref = bf16[128,512]{1,0:T(8,128)(2,1)S(1)} collective-permute-done((bf16[128,512]{1,0:T(8,128)(2,1)}, bf16[128,512]{1,0:T(8,128)(2,1)S(1)}, u32[]{:S(2)}, u32[]{:S(2)}) %collective-permute-start.16) | collective-permute-done | bytes 131104 | tf_op jit(solution)/shard_map/ppermute | solution.py:390
  119.0 4.4 %collective-permute-done.17.d_ref = bf16[128,512]{1,0:T(8,128)(2,1)S(1)} collective-permute-done((bf16[128,512]{1,0:T(8,128)(2,1)}, bf16[128,512]{1,0:T(8,128)(2,1)S(1)}, u32[]{:S(2)}, u32[]{:S(2)}) %collective-permute-start.17) | collective-permute-done | bytes 131104 | tf_op jit(solution)/shard_map/ppermute | solution.py:390
  123.4 0.6 copy-done.9
  124.0 2.0 mix.1.a_ref.mix_ref
  126.0 2.2 collective-permute-start.20
  128.2 3.2 %collective-permute-start.19 = (bf16[128,512]{1,0:T(8,128)(2,1)}, bf16[128,512]{1,0:T(8,128)(2,1)S(1)}, u32[]{:S(2)}, u32[]{:S(2)}) collective-permute-start(bf16[128,512]{1,0:T(8,128)(2,1)} %mix.1.a_ref.mix_ref), channel_id=1, source_target_pairs={{2,0},{3,1},{0,2},{1,3},{6,4},{7,5},{4,6},{5,7},{10,8},{11,9},{8,1... | collective-permute-start | bytes 393224 | tf_op jit(solution)/shard_map/ppermute | solution.py:405
  131.4 2.7 collective-permute-start.18
  134.1 1.9 slots.1
  136.0 3.4 %collective-permute-done.19.c_ref = bf16[128,512]{1,0:T(8,128)(2,1)S(1)} collective-permute-done((bf16[128,512]{1,0:T(8,128)(2,1)}, bf16[128,512]{1,0:T(8,128)(2,1)S(1)}, u32[]{:S(2)}, u32[]{:S(2)}) %collective-permute-start.19) | collective-permute-done | bytes 131104 | tf_op jit(solution)/shard_map/ppermute | solution.py:405
  139.4 0.9 collective-permute-done.18.b_ref
  140.3 0.6 copy-done.10
  141.0 5.0 %dispatch.1 = bf16[1024,2048]{1,0:T(8,128)(2,1)} custom-call(bf16[128,512]{1,0:T(8,128)(2,1)} %mix.1.a_ref.mix_ref, bf16[128,512]{1,0:T(8,128)(2,1)} %copy-done.10, bf16[128,512]{1,0:T(8,128)(2,1)} %copy-done.8, bf16[128,512]{1,0:T(8,128)(2,1)} %copy-done.6, f32[1,2048]{1,0:T(1,128)} %bitcast.47, bf16[1024,128]{1,0:T(8,128)(2,1)} %get-tuple-element.21.oh_ref), custom_call_target="tpu_custom_call" | custom-call | tf_op jit(solution)/shard_map/dispatch/pallas_call | solution.py:409
  146.0 9.8 %all-to-all-start.1 = ((bf16[64,16,2048]{2,1,0:T(8,128)(2,1)}), bf16[64,16,2048]{2,1,0:T(8,128)(2,1)}, u32[]{:S(2)}, u32[]{:S(2)}) async-start(bf16[64,16,2048]{2,1,0:T(8,128)(2,1)} %bitcast.35), calls=%async_computation.1 | async-start | bytes 8388608 | tf_op jit(solution)/shard_map/all_to_all | solution.py:420
  155.8 1.6 copy.33
  157.4 1.6 copy.34
  158.9 50.9 %all-to-all-done.1 = bf16[64,16,2048]{2,1,0:T(8,128)(2,1)} async-done(((bf16[64,16,2048]{2,1,0:T(8,128)(2,1)}), bf16[64,16,2048]{2,1,0:T(8,128)(2,1)}, u32[]{:S(2)}, u32[]{:S(2)}) %all-to-all-start.1) | async-done | bytes 4194336 | tf_op jit(solution)/shard_map/all_to_all | solution.py:420
  209.9 11.2 %expert.1 = bf16[1024,2048]{1,0:T(8,128)(2,1)} custom-call(bf16[1024,2048]{1,0:T(8,128)(2,1)} %bitcast.20.x_ref, bf16[2048,352]{1,0:T(8,128)(2,1)} %bitcast.37, bf16[2048,352]{1,0:T(8,128)(2,1)} %bitcast.38, bf16[352,2048]{1,0:T(8,128)(2,1)} %bitcast.39), custom_call_target="tpu_custom_call" | custom-call | tf_op jit(solution)/shard_map/expert/pallas_call | solution.py:422
  221.1 57.5 %all_to_all.16 = bf16[64,16,2048]{2,1,0:T(8,128)(2,1)} all-to-all(bf16[64,16,2048]{2,1,0:T(8,128)(2,1)} %bitcast.34), channel_id=1, replica_groups=mesh['seq'=64,'tensor'=4] {'seq'}, dimensions={0} | all-to-all | bytes 8388608 | tf_op jit(solution)/shard_map/all_to_all | solution.py:436
  278.6 4.2 %combine.1 = (bf16[128,512]{1,0:T(8,128)(2,1)}, bf16[128,512]{1,0:T(8,128)(2,1)}, bf16[128,512]{1,0:T(8,128)(2,1)}, bf16[128,512]{1,0:T(8,128)(2,1)}) custom-call(bf16[1024,2048]{1,0:T(8,128)(2,1)} %bitcast.36, bf16[1024,128]{1,0:T(8,128)(2,1)} %get-tuple-element.22.hi_ref, bf16[1024,128]{1,0:T(8,128)(2,1)} %get-tuple-element.23.lo_ref), custom_call_target="tpu_custom_call" | custom-call | tf_op jit(solution)/shard_map/combine/pallas_call | solution.py:437
  282.8 1.2 collective-permute-start.21
  284.1 4.1 %collective-permute-start.22 = (bf16[128,512]{1,0:T(8,128)(2,1)}, bf16[128,512]{1,0:T(8,128)(2,1)S(1)}, u32[]{:S(2)}, u32[]{:S(2)}) collective-permute-start(bf16[128,512]{1,0:T(8,128)(2,1)} %get-tuple-element.26), channel_id=1, source_target_pairs={{2,0},{3,1},{0,2},{1,3},{6,4},{7,5},{4,6},{5,7},{10,8},{11,9},{8,1... | collective-permute-start | bytes 393224 | tf_op jit(solution)/shard_map/ppermute | solution.py:390
  288.2 0.8 collective-permute-start.23
  289.0 1.0 constant_dynamic-slice_fusion
  290.0 0.7 copy.35
  290.7 1.5 collective-permute-done.21.b_ref
  292.2 8.0 %collective-permute-done.22.c_ref = bf16[128,512]{1,0:T(8,128)(2,1)S(1)} collective-permute-done((bf16[128,512]{1,0:T(8,128)(2,1)}, bf16[128,512]{1,0:T(8,128)(2,1)S(1)}, u32[]{:S(2)}, u32[]{:S(2)}) %collective-permute-start.22) | collective-permute-done | bytes 131104 | tf_op jit(solution)/shard_map/ppermute | solution.py:390
  300.2 1.0 collective-permute-done.23.d_ref
  301.2 0.6 copy-done.13
  301.9 1.9 finish.1
  (49 shorter events, 0.6 us)
Async XLA Ops:
  1.7 34.9 %collective-permute-start.9 = (bf16[128,576]{1,0:T(8,128)(2,1)S(1)}, bf16[128,576]{1,0:T(8,128)(2,1)S(1)}, u32[]{:S(2)}, u32[]{:S(2)}) collective-permute-start(bf16[128,576]{1,0:T(8,128)(2,1)S(1)} %bitcast.40), channel_id=1, source_target_pairs={{192,0},{196,4},{200,8},{204,12},{208,16},{212,20},{216,24},{220,2... | collective-permute-start | bytes 442376 | tf_op jit(solution)/shard_map/ppermute | solution.py:313
  3.8 34.6 %collective-permute-start.8 = (bf16[128,576]{1,0:T(8,128)(2,1)S(1)}, bf16[128,576]{1,0:T(8,128)(2,1)S(1)}, u32[]{:S(2)}, u32[]{:S(2)}) collective-permute-start(bf16[128,576]{1,0:T(8,128)(2,1)S(1)} %bitcast.41), channel_id=1, source_target_pairs={{128,0},{132,4},{136,8},{140,12},{144,16},{148,20},{152,24},{156,2... | collective-permute-start | bytes 442376 | tf_op jit(solution)/shard_map/ppermute | solution.py:313
  6.2 34.3 %collective-permute-start.7 = (bf16[128,576]{1,0:T(8,128)(2,1)S(1)}, bf16[128,576]{1,0:T(8,128)(2,1)S(1)}, u32[]{:S(2)}, u32[]{:S(2)}) collective-permute-start(bf16[128,576]{1,0:T(8,128)(2,1)S(1)} %bitcast.42), channel_id=1, source_target_pairs={{64,0},{68,4},{72,8},{76,12},{80,16},{84,20},{88,24},{92,28},{96,3... | collective-permute-start | bytes 442376 | tf_op jit(solution)/shard_map/ppermute | solution.py:313
  16.0 43.2 %collective-permute-start.6 = (bf16[128,384]{1,0:T(8,128)(2,1)}, bf16[128,384]{1,0:T(8,128)(2,1)S(1)}, u32[]{:S(2)}, u32[]{:S(2)}) collective-permute-start(bf16[128,384]{1,0:T(8,128)(2,1)} %get-tuple-element.15), channel_id=1, source_target_pairs={{56,0},{60,4},{32,8},{36,12},{40,16},{44,20},{48,24},{52,28},{24,3... | collective-permute-start | bytes 294920 | tf_op jit(solution)/shard_map/ppermute | solution.py:336
  18.7 3.8 %collective-permute-start = (bf16[128,384]{1,0:T(8,128)(2,1)}, bf16[128,384]{1,0:T(8,128)(2,1)S(1)}, u32[]{:S(2)}, u32[]{:S(2)}) collective-permute-start(bf16[128,384]{1,0:T(8,128)(2,1)} %get-tuple-element.15), channel_id=1, source_target_pairs={{8,0},{12,4},{16,8},{20,12},{24,16},{28,20},{0,24},{4,28},{40,32},... | collective-permute-start | bytes 294920 | tf_op jit(solution)/shard_map/ppermute | solution.py:336
  22.5 5.2 %collective-permute-start.1 = (bf16[128,384]{1,0:T(8,128)(2,1)}, bf16[128,384]{1,0:T(8,128)(2,1)S(1)}, u32[]{:S(2)}, u32[]{:S(2)}) collective-permute-start(bf16[128,384]{1,0:T(8,128)(2,1)} %get-tuple-element.15), channel_id=1, source_target_pairs={{16,0},{20,4},{24,8},{28,12},{0,16},{4,20},{8,24},{12,28},{48,32},... | collective-permute-start | bytes 294920 | tf_op jit(solution)/shard_map/ppermute | solution.py:336
  27.7 4.9 %collective-permute-start.2 = (bf16[128,384]{1,0:T(8,128)(2,1)}, bf16[128,384]{1,0:T(8,128)(2,1)S(1)}, u32[]{:S(2)}, u32[]{:S(2)}) collective-permute-start(bf16[128,384]{1,0:T(8,128)(2,1)} %get-tuple-element.15), channel_id=1, source_target_pairs={{24,0},{28,4},{0,8},{4,12},{8,16},{12,20},{16,24},{20,28},{56,32},... | collective-permute-start | bytes 294920 | tf_op jit(solution)/shard_map/ppermute | solution.py:336
  32.6 4.0 %collective-permute-start.3 = (bf16[128,384]{1,0:T(8,128)(2,1)}, bf16[128,384]{1,0:T(8,128)(2,1)S(1)}, u32[]{:S(2)}, u32[]{:S(2)}) collective-permute-start(bf16[128,384]{1,0:T(8,128)(2,1)} %get-tuple-element.15), channel_id=1, source_target_pairs={{32,0},{36,4},{40,8},{44,12},{48,16},{52,20},{56,24},{60,28},{0,32... | collective-permute-start | bytes 294920 | tf_op jit(solution)/shard_map/ppermute | solution.py:336
  36.6 6.1 %collective-permute-start.11 = (bf16[128,576]{1,0:T(8,128)(2,1)}, bf16[128,576]{1,0:T(8,128)(2,1)S(1)}, u32[]{:S(2)}, u32[]{:S(2)}) collective-permute-start(bf16[128,576]{1,0:T(8,128)(2,1)} %get-tuple-element.16), channel_id=1, source_target_pairs={{64,0},{68,4},{72,8},{76,12},{80,16},{84,20},{88,24},{92,28},{96,3... | collective-permute-start | bytes 442376 | tf_op jit(solution)/shard_map/ppermute | solution.py:313
  36.6 21.7 %collective-permute-start.5 = (bf16[128,384]{1,0:T(8,128)(2,1)}, bf16[128,384]{1,0:T(8,128)(2,1)}, u32[]{:S(2)}, u32[]{:S(2)}) collective-permute-start(bf16[128,384]{1,0:T(8,128)(2,1)} %get-tuple-element.15), channel_id=1, source_target_pairs={{48,0},{52,4},{56,8},{60,12},{32,16},{36,20},{40,24},{44,28},{16,3... | collective-permute-start | bytes 294920 | tf_op jit(solution)/shard_map/ppermute | solution.py:336
  38.4 19.0 %collective-permute-start.4 = (bf16[128,384]{1,0:T(8,128)(2,1)}, bf16[128,384]{1,0:T(8,128)(2,1)}, u32[]{:S(2)}, u32[]{:S(2)}) collective-permute-start(bf16[128,384]{1,0:T(8,128)(2,1)} %get-tuple-element.15), channel_id=1, source_target_pairs={{40,0},{44,4},{48,8},{52,12},{56,16},{60,20},{32,24},{36,28},{8,32... | collective-permute-start | bytes 294920 | tf_op jit(solution)/shard_map/ppermute | solution.py:336
  40.5 6.0 %collective-permute-start.12 = (bf16[128,576]{1,0:T(8,128)(2,1)}, bf16[128,576]{1,0:T(8,128)(2,1)}, u32[]{:S(2)}, u32[]{:S(2)}) collective-permute-start(bf16[128,576]{1,0:T(8,128)(2,1)} %get-tuple-element.16), channel_id=1, source_target_pairs={{128,0},{132,4},{136,8},{140,12},{144,16},{148,20},{152,24},{156,2... | collective-permute-start | bytes 442376 | tf_op jit(solution)/shard_map/ppermute | solution.py:313
  42.7 14.0 %copy-start = (bf16[512,576]{1,0:T(8,128)(2,1)}, bf16[512,576]{1,0:T(8,128)(2,1)S(1)}, u32[]{:S(2)}) copy-start(bf16[512,576]{1,0:T(8,128)(2,1)S(1)} %pad_maximum_fusion.pa_ref) | copy-start | bytes 1769476
  42.7 12.9 %collective-permute-start.13 = (bf16[128,576]{1,0:T(8,128)(2,1)}, bf16[128,576]{1,0:T(8,128)(2,1)S(1)}, u32[]{:S(2)}, u32[]{:S(2)}) collective-permute-start(bf16[128,576]{1,0:T(8,128)(2,1)} %get-tuple-element.16), channel_id=1, source_target_pairs={{192,0},{196,4},{200,8},{204,12},{208,16},{212,20},{216,24},{220,2... | collective-permute-start | bytes 442376 | tf_op jit(solution)/shard_map/ppermute | solution.py:313
  46.5 12.8 %collective-permute-start.10 = (bf16[512,576]{0,1:T(8,128)(2,1)S(1)}, bf16[512,576]{0,1:T(8,128)(2,1)S(1)}, u32[]{:S(2)}, u32[]{:S(2)}) collective-permute-start(bf16[512,576]{0,1:T(8,128)(2,1)S(1)} %copy.29), channel_id=1, source_target_pairs={{4,0},{0,4},{12,8},{8,12},{20,16},{16,20},{28,24},{24,28},{36,32},... | collective-permute-start | bytes 1769480 | tf_op jit(solution)/shard_map/ppermute | solution.py:315
  55.6 4.8 %copy-start.1 = (bf16[512,576]{1,0:T(8,128)(2,1)}, bf16[512,576]{1,0:T(8,128)(2,1)S(1)}, u32[]{:S(2)}) copy-start(bf16[512,576]{1,0:T(8,128)(2,1)S(1)} %constant_dynamic-update-slice_fusion.la_ref) | copy-start | bytes 1769476
  56.7 3.7 %collective-permute-start.14 = (bf16[512,576]{0,1:T(8,128)(2,1)}, bf16[512,576]{0,1:T(8,128)(2,1)}, u32[]{:S(2)}, u32[]{:S(2)}) collective-permute-start(bf16[512,576]{0,1:T(8,128)(2,1)} %copy.30), channel_id=1, source_target_pairs={{4,0},{0,4},{12,8},{8,12},{20,16},{16,20},{28,24},{24,28},{36,32},... | collective-permute-start | bytes 1769480 | tf_op jit(solution)/shard_map/ppermute | solution.py:315
  59.3 3.3 %copy-start.4 = (bf16[8,128,384]{2,1,0:T(8,128)(2,1)}, bf16[8,128,384]{2,1,0:T(8,128)(2,1)S(1)}, u32[]{:S(2)}) copy-start(bf16[8,128,384]{2,1,0:T(8,128)(2,1)S(1)} %bitcast_dynamic-update-slice_fusion.q_ref) | copy-start | bytes 2359300
  103.5 9.7 %collective-permute-start.15 = (bf16[128,512]{1,0:T(8,128)(2,1)}, bf16[128,512]{1,0:T(8,128)(2,1)S(1)}, u32[]{:S(2)}, u32[]{:S(2)}) collective-permute-start(bf16[128,512]{1,0:T(8,128)(2,1)} %get-tuple-element.18), channel_id=1, source_target_pairs={{3,0},{0,1},{1,2},{2,3},{7,4},{4,5},{5,6},{6,7},{11,8},{8,9},{9,10... | collective-permute-start | bytes 393224 | tf_op jit(solution)/shard_map/ppermute | solution.py:390
  106.5 12.5 %collective-permute-start.16 = (bf16[128,512]{1,0:T(8,128)(2,1)}, bf16[128,512]{1,0:T(8,128)(2,1)S(1)}, u32[]{:S(2)}, u32[]{:S(2)}) collective-permute-start(bf16[128,512]{1,0:T(8,128)(2,1)} %get-tuple-element.19), channel_id=1, source_target_pairs={{2,0},{3,1},{0,2},{1,3},{6,4},{7,5},{4,6},{5,7},{10,8},{11,9},{8,1... | collective-permute-start | bytes 393224 | tf_op jit(solution)/shard_map/ppermute | solution.py:390
  110.8 12.6 %collective-permute-start.17 = (bf16[128,512]{1,0:T(8,128)(2,1)}, bf16[128,512]{1,0:T(8,128)(2,1)S(1)}, u32[]{:S(2)}, u32[]{:S(2)}) collective-permute-start(bf16[128,512]{1,0:T(8,128)(2,1)} %get-tuple-element.20), channel_id=1, source_target_pairs={{1,0},{2,1},{3,2},{0,3},{5,4},{6,5},{7,6},{4,7},{9,8},{10,9},{11,1... | collective-permute-start | bytes 393224 | tf_op jit(solution)/shard_map/ppermute | solution.py:390
  113.2 10.2 %copy-start.5 = (bf16[128,512]{1,0:T(8,128)(2,1)}, bf16[128,512]{1,0:T(8,128)(2,1)S(1)}, u32[]{:S(2)}) copy-start(bf16[128,512]{1,0:T(8,128)(2,1)S(1)} %collective-permute-done.15.b_ref) | copy-start | bytes 393220
  119.0 4.4 %copy-start.7 = (bf16[128,512]{1,0:T(8,128)(2,1)}, bf16[128,512]{1,0:T(8,128)(2,1)S(1)}, u32[]{:S(2)}) copy-start(bf16[128,512]{1,0:T(8,128)(2,1)S(1)} %collective-permute-done.16.c_ref) | copy-start | bytes 393220
  123.4 0.7 copy-start.9
  126.0 9.9 %collective-permute-start.20 = (bf16[128,512]{1,0:T(8,128)(2,1)}, bf16[128,512]{1,0:T(8,128)(2,1)S(1)}, u32[]{:S(2)}, u32[]{:S(2)}) collective-permute-start(bf16[128,512]{1,0:T(8,128)(2,1)} %mix.1.a_ref.mix_ref), channel_id=1, source_target_pairs={{3,0},{0,1},{1,2},{2,3},{7,4},{4,5},{5,6},{6,7},{11,8},{8,9},{9,10... | collective-permute-start | bytes 393224 | tf_op jit(solution)/shard_map/ppermute | solution.py:405
  128.2 11.2 %collective-permute-start.19 = (bf16[128,512]{1,0:T(8,128)(2,1)}, bf16[128,512]{1,0:T(8,128)(2,1)S(1)}, u32[]{:S(2)}, u32[]{:S(2)}) collective-permute-start(bf16[128,512]{1,0:T(8,128)(2,1)} %mix.1.a_ref.mix_ref), channel_id=1, source_target_pairs={{2,0},{3,1},{0,2},{1,3},{6,4},{7,5},{4,6},{5,7},{10,8},{11,9},{8,1... | collective-permute-start | bytes 393224 | tf_op jit(solution)/shard_map/ppermute | solution.py:405
  131.4 8.9 %collective-permute-start.18 = (bf16[128,512]{1,0:T(8,128)(2,1)}, bf16[128,512]{1,0:T(8,128)(2,1)S(1)}, u32[]{:S(2)}, u32[]{:S(2)}) collective-permute-start(bf16[128,512]{1,0:T(8,128)(2,1)} %mix.1.a_ref.mix_ref), channel_id=1, source_target_pairs={{1,0},{2,1},{3,2},{0,3},{5,4},{6,5},{7,6},{4,7},{9,8},{10,9},{11,1... | collective-permute-start | bytes 393224 | tf_op jit(solution)/shard_map/ppermute | solution.py:405
  135.9 4.4 %copy-start.6 = (bf16[128,512]{1,0:T(8,128)(2,1)}, bf16[128,512]{1,0:T(8,128)(2,1)S(1)}, u32[]{:S(2)}) copy-start(bf16[128,512]{1,0:T(8,128)(2,1)S(1)} %collective-permute-done.20.d_ref) | copy-start | bytes 393220
  139.4 0.9 copy-start.8
  140.3 0.7 copy-start.10
  146.0 9.8 %copy-start.2 = (bf16[1,2048,352]{1,2,0:T(8,128)(2,1)S(1)}, bf16[1,2048,352]{1,2,0:T(8,128)(2,1)}, u32[]{:S(2)}) copy-start(bf16[1,2048,352]{1,2,0:T(8,128)(2,1)} %param.29) | copy-start | bytes 4325380
  146.0 63.9 %all-to-all-start.1 = ((bf16[64,16,2048]{2,1,0:T(8,128)(2,1)}), bf16[64,16,2048]{2,1,0:T(8,128)(2,1)}, u32[]{:S(2)}, u32[]{:S(2)}) async-start(bf16[64,16,2048]{2,1,0:T(8,128)(2,1)} %bitcast.35), calls=%async_computation.1 | async-start | bytes 8388608 | tf_op jit(solution)/shard_map/all_to_all | solution.py:420
  155.8 1.6 copy-start.3
  282.8 9.4 %collective-permute-start.21 = (bf16[128,512]{1,0:T(8,128)(2,1)}, bf16[128,512]{1,0:T(8,128)(2,1)S(1)}, u32[]{:S(2)}, u32[]{:S(2)}) collective-permute-start(bf16[128,512]{1,0:T(8,128)(2,1)} %get-tuple-element.25), channel_id=1, source_target_pairs={{3,0},{0,1},{1,2},{2,3},{7,4},{4,5},{5,6},{6,7},{11,8},{8,9},{9,10... | collective-permute-start | bytes 393224 | tf_op jit(solution)/shard_map/ppermute | solution.py:390
  284.1 16.2 %collective-permute-start.22 = (bf16[128,512]{1,0:T(8,128)(2,1)}, bf16[128,512]{1,0:T(8,128)(2,1)S(1)}, u32[]{:S(2)}, u32[]{:S(2)}) collective-permute-start(bf16[128,512]{1,0:T(8,128)(2,1)} %get-tuple-element.26), channel_id=1, source_target_pairs={{2,0},{3,1},{0,2},{1,3},{6,4},{7,5},{4,6},{5,7},{10,8},{11,9},{8,1... | collective-permute-start | bytes 393224 | tf_op jit(solution)/shard_map/ppermute | solution.py:390
  288.2 13.0 %collective-permute-start.23 = (bf16[128,512]{1,0:T(8,128)(2,1)}, bf16[128,512]{1,0:T(8,128)(2,1)S(1)}, u32[]{:S(2)}, u32[]{:S(2)}) collective-permute-start(bf16[128,512]{1,0:T(8,128)(2,1)} %get-tuple-element.27), channel_id=1, source_target_pairs={{1,0},{2,1},{3,2},{0,3},{5,4},{6,5},{7,6},{4,7},{9,8},{10,9},{11,1... | collective-permute-start | bytes 393224 | tf_op jit(solution)/shard_map/ppermute | solution.py:390
  292.2 9.0 %copy-start.11 = (bf16[128,512]{1,0:T(8,128)(2,1)}, bf16[128,512]{1,0:T(8,128)(2,1)S(1)}, u32[]{:S(2)}) copy-start(bf16[128,512]{1,0:T(8,128)(2,1)S(1)} %collective-permute-done.21.b_ref) | copy-start | bytes 393220
  300.2 1.0 copy-start.12
  301.2 0.7 copy-start.13
where the time goes:
time: 305 us; the launch traced here: 304 us
  waiting for transfers between devices  88.9 us (29%)
  blocking collectives  74 us (24%)
  starting transfers between devices  62.9 us (21%)
  Pallas kernels  55 us (18%)
  local copies, waits for them, and re-layouts  21.5 us (7%)
    all_to_all x1, blocking collectives, local(): lax.all_to_all(results.reshape(seq_count, SLOTS, d), 'seq', 0, 0, tiled=T...  57.5 us
    all_to_all x1, waiting for transfers between devices, local(): lax.all_to_all(outbound.reshape(seq_count, SLOTS, d), 'seq', 0, 0, tiled=...  50.9 us
    pallas_call x1, Pallas kernels, local(): pl.pallas_call(attend_kernel, out_shape=jax.ShapeDtypeStruct((m, n, 3 * V...  21.5 us
    ppermute x6, waiting for transfers between devices, exchange(): lax.ppermute(parts[j], 'tensor', tensor_from(-j, tensor_count))  20.7 us
    all_to_all x1, blocking collectives, local(): lax.all_to_all(partial, 'seq', 0, 0, tiled=True, axis_index_groups=zy_gro...  16.5 us
    unnamed x43, local copies, waits for them, and re-layouts  16 us
    ppermute x6, starting transfers between devices, exchange(): lax.ppermute(parts[j], 'tensor', tensor_from(-j, tensor_count))  15.8 us
    ppermute x7, starting transfers between devices, local(): lax.ppermute(query, 'seq', seq_perm(0, dz, dy, 0))  12.4 us
  transfers between devices with their start and end apart: 25, of which 12 were waited for; matrix products, arithmetic and copies ran while one was open for 6% of the time, Pallas kernels for 2%

commit v1 on v0

v1 whole, which is shorter than its diff:
```python
import functools

import jax
import jax.numpy as jnp
import numpy as np
from jax import lax
from jax.experimental import pallas as pl
from jax.experimental.pallas import tpu as pltpu
from jax.sharding import PartitionSpec as P


NOPE = 128
ROPE = 64
VDIM = 128
LATENT = 512
KEY = LATENT + ROPE
SLOTS = 16
EPSILON = 1e-06
ROPE_BASE = 50000.0
MASKED = -1e30

NX, NZ, NY, NC = 4, 2, 4, 2
BF = jnp.bfloat16
F32 = jnp.float32
NT = (((1,), (1,)), ((), ()))
VM = pltpu.MemorySpace.VMEM
SM = pltpu.MemorySpace.SMEM


def seq_id(x, z, y, c):
    return (((x % NX) * NZ + z % NZ) * NY + y % NY) * NC + c % NC


def seq_perm(dx, dz, dy, dc):
    pairs = []
    for x in range(NX):
        for z in range(NZ):
            for y in range(NY):
                for c in range(NC):
                    pairs.append((seq_id(x + dx, z + dz, y + dy, c + dc), seq_id(x, z, y, c)))
    return pairs


def tensor_from(d, n):
    return [((t + d) % n, t) for t in range(n)]


def zy_groups():
    return [
        [seq_id(x, z, y, c) for z in range(NZ) for y in range(NY)]
        for x in range(NX)
        for c in range(NC)
    ]


def my_place():
    s = lax.axis_index("seq")
    c = lax.rem(s, NC)
    y = lax.rem(lax.div(s, NC), NY)
    z = lax.rem(lax.div(s, NC * NY), NZ)
    x = lax.div(s, NC * NY * NZ)
    return x, z, y, c


def dot(a, b, dims=(((1,), (0,)), ((), ()))):
    return lax.dot_general(a, b, dims, preferred_element_type=F32)


def token_rows(tok, lengths, group):
    tok = tok.astype(F32)
    start = jnp.zeros_like(tok)
    grp = jnp.zeros_like(tok)
    end = jnp.int32(0)
    for r in range(lengths.shape[0]):
        begin = end
        end = end + lengths[r]
        ef = end.astype(F32)
        bf = begin.astype(F32)
        past = tok >= ef
        start = jnp.where(past, ef, start)
        if group is not None:
            inside = jnp.logical_and(tok >= bf, tok < ef)
            grp = jnp.where(inside, group[r].astype(F32), grp)
    return tok, start, grp


def to_columns(rows, n):
    which = lax.broadcasted_iota(jnp.int32, (n, n), 0)
    out = jnp.zeros((n, n), F32)
    for i, row in enumerate(rows):
        out = jnp.where(which == i, jnp.broadcast_to(row, (n, n)), out)
    return out.T


def project_kernel(prefix, lengths, tok_ref, fcol_ref, frow_ref, hid_ref, gain_ref, wq_ref, wl_ref, kvg_ref, q_ref, lat_ref):
    n = hid_ref.shape[0]
    half = ROPE // 2
    s = lax.axis_index("seq")
    tok, start, _ = token_rows(tok_ref[pl.ds(s, 1), :], lengths, None)
    position = tok - start + float(prefix)
    hid = hid_ref[...].astype(F32)
    scale = lax.rsqrt(jnp.mean(hid * hid, axis=-1, keepdims=True) + EPSILON)
    normed = (hid * scale * gain_ref[...]).astype(BF)

    angles = to_columns([position], n)[:, 0:1] * frow_ref[...]
    lane = lax.broadcasted_iota(jnp.int32, (n, 2 * ROPE), 1)
    first = lax.rem(lane, ROPE) < half
    cos = jnp.cos(angles)
    sin = jnp.sin(angles)
    query = dot(normed, wq_ref[...]).astype(BF)
    width = NOPE + ROPE
    pe = jnp.concatenate([query[:, NOPE:width], query[:, width + NOPE : 2 * width]], axis=1).astype(F32)
    partner = jnp.where(first, -pltpu.roll(pe, 2 * ROPE - half, 1), pltpu.roll(pe, half, 1))
    pe = (pe * cos + partner * sin).astype(BF)
    for i in range(q_ref.shape[0]):
        q_ref[i, :, 0:NOPE] = query[:, 0:NOPE]
        q_ref[i, :, NOPE : 2 * NOPE] = query[:, width : width + NOPE]
        q_ref[i, :, 2 * NOPE :] = pe

    raw = dot(wl_ref[...], normed, NT)
    lat = raw[:LATENT]
    lscale = lax.rsqrt(jnp.mean(lat * lat, axis=0, keepdims=True) + EPSILON)
    for i in range(0, LATENT, n):
        gain = jnp.broadcast_to(kvg_ref[:, i : i + n], (n, n)).T
        lat_ref[i : i + n, :] = (lat[i : i + n] * lscale * gain).astype(BF)
    angles = fcol_ref[...] * position
    cos = jnp.cos(angles)
    sin = jnp.sin(angles)
    top, low = raw[LATENT : LATENT + half], raw[LATENT + half :]
    lat_ref[LATENT : LATENT + half, :] = (top * cos - low * sin).astype(BF)
    lat_ref[LATENT + half :, :] = (low * cos + top * sin).astype(BF)


def attend_kernel(
    lengths, group, table, tok_ref, q_ref, pa_ref, pb_ref, la_ref, lb_ref, ku_ref, vu_ref,
    out_ref, s_ref, qf_ref, owner,
):
    j = pl.program_id(0)
    n = q_ref.shape[1]
    x, z, y, c = my_place()

    @pl.when(j == 0)
    def _():
        for g in range(table.shape[0]):
            for i in range(table.shape[1]):
                owner[table[g, i]] = g

    me = seq_id(x, lax.div(j, NY), lax.rem(j, NY), c)
    tok, start, grp = token_rows(tok_ref[pl.ds(me, 1), :], lengths, group)
    cols = to_columns([tok, start, grp], n)
    two = jnp.concatenate([cols, cols], axis=0)
    pos_q, start_q, grp_q = two[:, 0:1], two[:, 1:2], two[:, 2:3]

    for h in range(2):
        up = ku_ref[:, h * NOPE : (h + 1) * NOPE]
        nope = q_ref[0, :, h * NOPE : (h + 1) * NOPE]
        qf_ref[h * n : (h + 1) * n, :LATENT] = dot(nope, up, NT).astype(BF)
        qf_ref[h * n : (h + 1) * n, LATENT:] = q_ref[0, :, 2 * NOPE + h * ROPE : 2 * NOPE + (h + 1) * ROPE]
    qf = qf_ref[...]
    keys = (pa_ref, pb_ref, la_ref, lb_ref)
    high = jnp.full((2 * n, 1), MASKED, F32)
    for b, k_ref in enumerate(keys):
        sc = dot(qf, k_ref[...])
        for i in range(NX):
            holder = seq_id(x + i, z, y, c + b % 2)
            part = sc[:, i * n : (i + 1) * n]
            if b < 2:
                part = part + jnp.where(grp_q == owner[holder].astype(F32), 0.0, MASKED)
            else:
                pos_k = tok_ref[pl.ds(holder, 1), :].astype(F32)
                seen = jnp.logical_and(pos_k >= start_q, pos_k <= pos_q)
                part = jnp.where(seen, part, MASKED)
            s_ref[:, (b * NX + i) * n : (b * NX + i + 1) * n] = part
            high = jnp.maximum(high, jnp.max(part, axis=-1, keepdims=True))
    scale = (NOPE + ROPE) ** (-0.5)
    log2e = 1.4426950408889634
    top = jnp.where(high > 0.5 * MASKED, high, 0.0)
    den = jnp.zeros((2 * n, 1), F32)
    acc = jnp.zeros((2 * n, LATENT), F32)
    width = NX * n
    for b, k_ref in enumerate(keys):
        w = jnp.exp2((s_ref[:, b * width : (b + 1) * width] - top) * (scale * log2e))
        den = den + jnp.sum(w, axis=-1, keepdims=True)
        acc = acc + dot(w.astype(BF), k_ref[:LATENT, :], NT)
    some = den > 0.0
    att = (acc / jnp.where(some, den, 1.0)).astype(BF)
    lse = jnp.where(some, top * scale + jnp.log(jnp.where(some, den, 1.0)), MASKED)
    hi = lse.astype(BF).astype(F32)
    mid = (lse - hi).astype(BF).astype(F32)
    low = lse - hi - mid
    lane = lax.broadcasted_iota(jnp.int32, (n, 128), 1)
    stat = jnp.zeros((n, 128), F32)
    for h in range(2):
        rows = slice(h * n, (h + 1) * n)
        out_ref[0, :, h * VDIM : (h + 1) * VDIM] = dot(
            att[rows], vu_ref[:, h * VDIM : (h + 1) * VDIM]
        ).astype(BF)
        for i, term in enumerate((hi, mid, low)):
            stat = jnp.where(lane == 3 * h + i, term[rows], stat)
    out_ref[0, :, 2 * VDIM :] = stat.astype(BF)


def merge_kernel(got_ref, out_ref):
    m = got_ref.shape[0]
    for h in range(2):
        lse = []
        for i in range(m):
            st = got_ref[i, :, 2 * VDIM :].astype(F32)
            lse.append(st[:, 3 * h : 3 * h + 1] + st[:, 3 * h + 1 : 3 * h + 2] + st[:, 3 * h + 2 : 3 * h + 3])
        top = functools.reduce(jnp.maximum, lse)
        den = jnp.zeros_like(top)
        acc = jnp.zeros((got_ref.shape[1], VDIM), F32)
        for i in range(m):
            w = jnp.exp(lse[i] - top)
            den = den + w
            acc = acc + w * got_ref[i, :, h * VDIM : (h + 1) * VDIM].astype(F32)
        out_ref[:, h * VDIM : (h + 1) * VDIM] = (acc / den).astype(BF)


def finish_kernel(mix_ref, a_ref, b_ref, c_ref, d_ref, out_ref):
    total = a_ref[...].astype(F32) + b_ref[...].astype(F32) + c_ref[...].astype(F32) + d_ref[...].astype(F32)
    out_ref[...] = (mix_ref[...].astype(F32) + total).astype(BF)


def slots_kernel(ids_ref, gates_ref, oh_ref, hi_ref, lo_ref):
    experts = oh_ref.shape[0] // SLOTS
    n = oh_ref.shape[1]
    which = lax.broadcasted_iota(jnp.int32, (experts, n), 0)
    named = jnp.zeros((experts, n), F32)
    gate = jnp.zeros((experts, n), F32)
    for k in range(ids_ref.shape[0]):
        hit = which == ids_ref[k : k + 1, :]
        named = jnp.where(hit, 1.0, named)
        gate = jnp.where(hit, gates_ref[k : k + 1, :], gate)
    before = lax.broadcasted_iota(jnp.int32, (n, n), 0) < lax.broadcasted_iota(jnp.int32, (n, n), 1)
    count = dot(named.astype(BF), jnp.where(before, 1.0, 0.0).astype(BF))
    slot = jnp.where(named > 0.0, count, -1.0)
    ghi = gate.astype(BF).astype(F32)
    glo = gate - ghi
    level = lax.broadcasted_iota(jnp.int32, (SLOTS, n), 0).astype(F32)
    for e in range(experts):
        hit = slot[e : e + 1, :] == level
        rows = slice(e * SLOTS, (e + 1) * SLOTS)
        oh_ref[rows, :] = jnp.where(hit, 1.0, 0.0).astype(BF)
        hi_ref[rows, :] = jnp.where(hit, ghi[e : e + 1, :], 0.0).astype(BF)
        lo_ref[rows, :] = jnp.where(hit, glo[e : e + 1, :], 0.0).astype(BF)


def dispatch_kernel(v0, v1, v2, v3, hid_ref, wo_ref, wa_ref, wb_ref, gain_ref, oh_ref, out_ref, mix_ref, in_ref, acc_ref):
    d = hid_ref.shape[1]
    w = wa_ref.shape[2]
    q = mix_ref.shape[1]
    x, _, _, c = my_place()
    t = lax.axis_index("tensor")

    @pl.when(pl.program_id(0) == 0)
    def _():
        first = v0[...]
        others = (v1[...], v2[...], v3[...])
        for i in range(NX):
            for b, ref in enumerate((wa_ref, wb_ref)):
                col = pl.multiple_of((lax.rem(x + i, NX) * NC + lax.rem(c + b, NC)) * w, w)
                total = dot(first, wo_ref[:, pl.ds(col, w)])
                for j, v in enumerate(others):
                    total = total + dot(v, ref[i * len(others) + j])
                acc_ref[:, pl.ds(col, w)] = (hid_ref[:, pl.ds(col, w)].astype(F32) + total).astype(BF)
        mix_ref[...] = acc_ref[:, pl.ds(pl.multiple_of(t * q, q), q)]
        mixed = acc_ref[...].astype(F32)
        scale = lax.rsqrt(jnp.sum(mixed * mixed, axis=-1, keepdims=True) / d + EPSILON)
        in_ref[...] = (mixed * scale * gain_ref[...]).astype(BF)

    out_ref[...] = dot(oh_ref[...], in_ref[...]).astype(BF)


def expert_kernel(x_ref, wgu_ref, wd_ref, out_ref):
    hid = wd_ref.shape[0]
    wide = wgu_ref.shape[1] // 2
    both = dot(x_ref[...], wgu_ref[...])
    gate, up = both[:, :wide], both[:, wide:]
    act = (gate / (1.0 + jnp.exp(-gate)) * up).astype(BF)[:, :hid]
    out_ref[...] = dot(act, wd_ref[...]).astype(BF)


def combine_kernel(place, rows_ref, hi_ref, lo_ref, out_ref):
    tn = (((0,), (0,)), ((), ()))
    out_ref[...] = (dot(hi_ref[...], rows_ref[...], tn) + dot(lo_ref[...], rows_ref[...], tn)).astype(BF)


def whole(n):
    return [pl.BlockSpec(memory_space=VM)] * n


def local(
    hidden, attn_gain, w_query, w_latent_down, kv_gain, w_key_up, w_value_up, w_out, ffn_gain,
    w_gate_exp, w_up_exp, w_down_exp, page_pool, page_table, request_group, suffix_lengths,
    token_order, expert_ids, expert_gates,
):
    seq_count = lax.axis_size("seq")
    tensor_count = lax.axis_size("tensor")
    tensor_index = lax.axis_index("tensor")
    n, d = hidden.shape
    quarter = d // tensor_count
    prefix = page_table.shape[1] * page_pool.shape[1]
    tok = token_order.reshape(seq_count, n)
    params = pltpu.CompilerParams(vmem_limit_bytes=56 << 20)

    m = NZ * NY

    def spread(piece):
        got = [lax.ppermute(piece, "seq", seq_perm(i, 0, 0, 0)) for i in range(1, NX)]
        own = jnp.concatenate([piece] + got, axis=1)
        return own, lax.ppermute(own, "seq", seq_perm(0, 0, 0, 1))

    pages_a, pages_b = spread(page_pool[0].T)

    freq = ROPE_BASE ** (-2.0 * np.arange(ROPE // 2, dtype=np.float64) / ROPE)
    query, latent = pl.pallas_call(
        functools.partial(project_kernel, prefix),
        out_shape=(
            jax.ShapeDtypeStruct((m, n, w_query.shape[1]), BF),
            jax.ShapeDtypeStruct((KEY, n), BF),
        ),
        in_specs=[pl.BlockSpec(memory_space=SM)] + whole(8),
        out_specs=tuple(whole(2)),
        compiler_params=params,
        name="project",
    )(
        suffix_lengths, tok, jnp.asarray(freq[:, None], F32), jnp.asarray(np.tile(freq, 4)[None, :], F32), hidden,
        attn_gain.reshape(1, d), w_query, w_latent_down.T, kv_gain.reshape(1, LATENT),
    )

    lat_a, lat_b = spread(latent)
    queries = lax.all_to_all(query, "seq", 0, 0, tiled=True, axis_index_groups=zy_groups())

    x, _, _, c = my_place()
    share = d // (NX * NC)
    mine = lax.dynamic_slice_in_dim(w_out, (x * NC + c) * share, share, 1)
    other = jnp.stack([lax.ppermute(mine, "tensor", tensor_from(j, tensor_count)) for j in range(1, tensor_count)])
    wide = [other] + [lax.ppermute(other, "seq", seq_perm(i, 0, 0, 0)) for i in range(1, NX)]

    oh, ghi, glo = pl.pallas_call(
        slots_kernel,
        out_shape=(jax.ShapeDtypeStruct((seq_count * SLOTS, n), BF),) * 3,
        in_specs=whole(2),
        out_specs=tuple(whole(3)),
        compiler_params=params,
        name="slots",
    )(expert_ids.T, expert_gates.T)

    keys = NX * n

    def fixed(shape):
        return pl.BlockSpec(shape, lambda j, *_: (0,) * len(shape))

    partial = pl.pallas_call(
        attend_kernel,
        out_shape=jax.ShapeDtypeStruct((m, n, 3 * VDIM), BF),
        grid_spec=pltpu.PrefetchScalarGridSpec(
            num_scalar_prefetch=3,
            grid=(m,),
            in_specs=[fixed(tok.shape)]
            + [pl.BlockSpec((1,) + query.shape[1:], lambda j, *_: (j, 0, 0))]
            + [fixed((KEY, keys))] * 4
            + [fixed(w_key_up.shape), fixed(w_value_up.shape)],
            out_specs=pl.BlockSpec((1, n, 3 * VDIM), lambda j, *_: (j, 0, 0)),
            scratch_shapes=[
                pltpu.VMEM((2 * n, 4 * keys), F32),
                pltpu.VMEM((2 * n, KEY), BF),
                pltpu.SMEM((seq_count,), jnp.int32),
            ],
        ),
        compiler_params=params,
        name="attend",
    )(
        suffix_lengths, request_group, page_table, tok, queries, pages_a, pages_b, lat_a, lat_b, w_key_up, w_value_up
    )

    got = lax.all_to_all(partial, "seq", 0, 0, tiled=True, axis_index_groups=zy_groups())
    values = pl.pallas_call(
        merge_kernel,
        out_shape=jax.ShapeDtypeStruct((n, 2 * VDIM), BF),
        in_specs=whole(1),
        out_specs=whole(1)[0],
        compiler_params=params,
        name="merge",
    )(got)
    all_values = [values] + [
        lax.ppermute(values, "tensor", tensor_from(j, tensor_count)) for j in range(1, tensor_count)
    ]
    wide, _ = lax.optimization_barrier((wide, values))
    wide = jnp.concatenate(wide, axis=0)
    wide_b = lax.ppermute(wide, "seq", seq_perm(0, 0, 0, 1))

    piece = jax.ShapeDtypeStruct((n, quarter), BF)
    rows = seq_count * SLOTS
    block = rows // 4
    outbound, mixed = pl.pallas_call(
        dispatch_kernel,
        out_shape=(jax.ShapeDtypeStruct((rows, d), BF), piece),
        grid=(rows // block,),
        in_specs=[fixed(values.shape)] * 4
        + [fixed(hidden.shape), fixed(w_out.shape), fixed(wide.shape), fixed(wide.shape), fixed((1, d))]
        + [pl.BlockSpec((block, n), lambda i: (i, 0))],
        out_specs=(pl.BlockSpec((block, d), lambda i: (i, 0)), fixed((n, quarter))),
        scratch_shapes=[pltpu.VMEM((n, d), BF), pltpu.VMEM((n, d), BF)],
        compiler_params=params,
        name="dispatch",
    )(*all_values, hidden, w_out, wide, wide_b, ffn_gain.reshape(1, d), oh)
    arrived = lax.all_to_all(outbound.reshape(seq_count, SLOTS, d), "seq", 0, 0, tiled=True)
    hid = w_gate_exp.shape[2]
    fill = jnp.zeros((d, -hid % 128), BF)
    both = jnp.concatenate([w_gate_exp[0], fill, w_up_exp[0], fill], axis=1)
    results = pl.pallas_call(
        expert_kernel,
        out_shape=jax.ShapeDtypeStruct((rows, d), BF),
        grid=(rows // block,),
        in_specs=[pl.BlockSpec((block, d), lambda i: (i, 0)), fixed(both.shape), fixed((hid, d))],
        out_specs=pl.BlockSpec((block, d), lambda i: (i, 0)),
        compiler_params=params,
        name="expert",
    )(arrived.reshape(rows, d), both, w_down_exp[0])
    back = lax.all_to_all(results.reshape(seq_count, SLOTS, d), "seq", 0, 0, tiled=True)
    place = tensor_index.astype(jnp.int32).reshape(1)

    def combined(i):
        return pl.pallas_call(
            combine_kernel,
            out_shape=piece,
            grid_spec=pltpu.PrefetchScalarGridSpec(
                num_scalar_prefetch=1,
                grid=(1,),
                in_specs=[
                    pl.BlockSpec((rows, quarter), lambda j, place: (0, lax.rem(place[0] + i, tensor_count))),
                    fixed(ghi.shape),
                    fixed(glo.shape),
                ],
                out_specs=fixed((n, quarter)),
            ),
            compiler_params=params,
            name="combine",
        )(place, back.reshape(rows, d), ghi, glo)

    sums = [None] * tensor_count
    for i in (2, 1, 3):
        sums[i] = lax.ppermute(combined(i), "tensor", tensor_from(-i, tensor_count))
    sums[0] = combined(0)
    hidden_out = pl.pallas_call(
        finish_kernel, out_shape=piece, in_specs=whole(5), out_specs=whole(1)[0], compiler_params=params, name="finish"
    )(mixed, *sums)
    width = KEY // tensor_count
    cache_part = lax.dynamic_slice_in_dim(latent, tensor_index * width, width, 0).T
    return (hidden_out, cache_part)


def solution(mesh):
    placed = (
        P("seq", None),
        P(),
        P(None, "tensor"),
        P(),
        P(),
        P(None, "tensor"),
        P(None, "tensor"),
        P("tensor", None),
        P(),
        P("seq", None, "tensor"),
        P("seq", None, "tensor"),
        P("seq", "tensor", None),
        P("seq", None, None),
        P(),
        P(),
        P(),
        P(),
        P("seq", None),
        P("seq", None),
    )

    return jax.shard_map(
        local,
        mesh=mesh,
        in_specs=placed,
        out_specs=(P("seq", "tensor"), P("seq", "tensor")),
        check_vma=False,
    )
```

time: 305 us -> 290 us (0.951)
  blocking collectives: 74 us -> 0 us
  waiting for transfers between devices: 88.9 us -> 146 us
  local copies, waits for them, and re-layouts: 21.5 us -> 8.98 us
  Pallas kernels: 55 us -> 61.5 us
  starting transfers between devices: 62.9 us -> 68.1 us
    all_to_all x2 -> x0, blocking collectives: 74 us -> none  [the longest x1 57.5 us: local(): lax.all_to_all(results.reshape(seq_count, SLOTS, d), 'seq', 0, 0, tiled=T...]
    all_to_all x0 -> x3, waiting for transfers between devices: none -> 54.1 us  [the longest x1 54.1 us: local(): lax.all_to_all(results.reshape(seq_count, SLOTS, d), 'seq', 0, 0, tiled=T...]
    all_to_all x0 -> x3, starting transfers between devices: none -> 17.5 us  [the longest x1 6.5 us: local(): lax.all_to_all(query, 'seq', 0, 0, tiled=True, axis_index_groups=zy_group...]
    unnamed x43 -> x48, local copies, waits for them, and re-layouts: 16 us -> 7.32 us
    ppermute x16 -> x13, starting transfers between devices: 36.4 us -> 29.8 us  [the longest x3 9.66 us: local(): lax.ppermute(mine, 'tensor', tensor_from(j, tensor_count))]
    pallas_call x4 -> x6, Pallas kernels: 14.2 us -> 19.7 us  [the longest x4 9.95 us: combined(): pl.pallas_call(combine_kernel, out_shape=piece, grid_spec=pltpu.PrefetchS...]
    ppermute x2, starting transfers between devices: 8.83 us -> 5.22 us  [spread(): return (own, lax.ppermute(own, 'seq', seq_perm(0, 0, 0, 1)))]
    ppermute x2 -> x0, local copies, waits for them, and re-layouts: 3.24 us -> none  [spread(): return (own, lax.ppermute(own, 'seq', seq_perm(0, 0, 0, 1)))]
  transfers between devices with their start and end apart: 25 -> 25, of which waited for: 12 -> 14; matrix products, arithmetic and copies ran while one was open for 6% -> 3% of each run, Pallas kernels for 2% -> 2%
where the time goes in v1:
time: 290 us; the launch traced here: 289 us
  waiting for transfers between devices  146 us (50%)
  starting transfers between devices  68.1 us (23%)
  Pallas kernels  61.5 us (21%)
  local copies, waits for them, and re-layouts  8.98 us (3%)
  other arithmetic  3.24 us (1%)
    all_to_all x1, waiting for transfers between devices, local(): lax.all_to_all(results.reshape(seq_count, SLOTS, d), 'seq', 0, 0, tiled=T...  54.1 us
    all_to_all x1, waiting for transfers between devices, local(): lax.all_to_all(outbound.reshape(seq_count, SLOTS, d), 'seq', 0, 0, tiled=...  48.1 us
    pallas_call x1, Pallas kernels, local(): pl.pallas_call(attend_kernel, out_shape=jax.ShapeDtypeStruct((m, n, 3 * V...  21.3 us
    ppermute x3, waiting for transfers between devices, local(): lax.ppermute(mine, 'tensor', tensor_from(j, tensor_count))  13 us
    ppermute x3, waiting for transfers between devices, local(): lax.ppermute(other, 'seq', seq_perm(i, 0, 0, 0))  12.4 us
    pallas_call x1, Pallas kernels, local(): pl.pallas_call(expert_kernel, out_shape=jax.ShapeDtypeStruct((rows, d), B...  12.3 us
    pallas_call x4, Pallas kernels, combined(): pl.pallas_call(combine_kernel, out_shape=piece, grid_spec=pltpu.PrefetchS...  9.95 us
    ppermute x3, starting transfers between devices, local(): lax.ppermute(mine, 'tensor', tensor_from(j, tensor_count))  9.66 us
  transfers between devices with their start and end apart: 25, of which 14 were waited for; matrix products, arithmetic and copies ran while one was open for 3% of the time, Pallas kernels for 2%

profile of v1, /device:TPU:1, one launch (start us, length us, event | category | flops | bytes accessed | tf_op | source)
XLA Modules:
  0.0 288.9 jit_solution(3975731202515033180)
XLA Ops:
  0.6 4.4 %project.1 = (bf16[8,128,384]{2,1,0:T(8,128)(2,1)}, bf16[576,128]{1,0:T(8,128)(2,1)}) custom-call(s32[16]{0:T(128)} %lengths.3, s32[64,128]{1,0:T(8,128)} %bitcast.33, f32[32,1]{1,0:T(8,128)} %constant.34.clone.fcol_ref, f32[1,128]{1,0:T(1,128)} %constant.35.clone.frow_ref, bf16[128,2048]{1,0:T(8,128)(2,1)} %hid_ref.3, f32[1,2048]{1,0:T(1,128)} %bitcast.38, ...), custom_call_target="tpu_custom_call" | custom-call | tf_op jit(solution)/shard_map/project/pallas_call | solution.py:317
  5.1 6.5 %all-to-all-start = ((bf16[8,128,384]{2,1,0:T(8,128)(2,1)}), bf16[8,128,384]{2,1,0:T(8,128)(2,1)S(1)}, u32[]{:S(2)}, u32[]{:S(2)}) async-start(bf16[8,128,384]{2,1,0:T(8,128)(2,1)} %get-tuple-element.13), calls=%async_computation | async-start | bytes 1572864 | tf_op jit(solution)/shard_map/all_to_all | solution.py:333
  11.6 1.3 collective-permute-start.2
  12.9 2.4 collective-permute-start.1
  15.3 1.2 collective-permute-start
  16.5 0.3 collective-permute-start.6
  16.8 2.4 collective-permute-start.4
  19.2 0.1 collective-permute-start.5
  19.3 2.2 collective-permute-done.1
  21.5 0.1 pad_maximum_fusion.1.pa_ref
  21.6 3.3 %collective-permute-start.3 = (bf16[576,512]{1,0:T(8,128)(2,1)S(1)}, bf16[576,512]{1,0:T(8,128)(2,1)S(1)}, u32[]{:S(2)}, u32[]{:S(2)}) collective-permute-start(bf16[576,512]{1,0:T(8,128)(2,1)S(1)} %pad_maximum_fusion.1.pa_ref), channel_id=1, source_target_pairs={{4,0},{0,4},{12,8},{8,12},{20,16},{16,20},{28,24},{24,28},{36,32},... | collective-permute-start | bytes 1769480 | tf_op jit(solution)/shard_map/ppermute | solution.py:312
  24.9 2.9 collective-permute-done.5
  27.9 1.9 collective-permute-start.7
  29.8 1.6 collective-permute-done.7.lb_ref
  31.4 0.8 copy-done.8
  32.3 0.9 copy-done
  33.1 21.3 %attend.1 = bf16[8,128,384]{2,1,0:T(8,128)(2,1)} custom-call(s32[16]{0:T(128)} %lengths.3, s32[16]{0:T(128)} %group.1, s32[4,16]{1,0:T(4,128)} %table.1, s32[64,128]{1,0:T(8,128)} %bitcast.34, bf16[8,128,384]{2,1,0:T(8,128)(2,1)} %copy-done, bf16[576,512]{1,0:T(8,128)(2,1)} %copy-done.3, bf16[576,512]{1,0:T(8,128)(2,1)} %copy-done.7, ...), custom_call_target="tpu_custom_call" | custom-call | tf_op jit(solution)/shard_map/attend/pallas_call | solution.py:355
  54.4 5.1 %all-to-all-start.1 = ((bf16[8,128,384]{2,1,0:T(8,128)(2,1)}), bf16[8,128,384]{2,1,0:T(8,128)(2,1)S(1)}, u32[]{:S(2)}, u32[]{:S(2)}) async-start(bf16[8,128,384]{2,1,0:T(8,128)(2,1)} %attend.1), calls=%async_computation.1 | async-start | bytes 1572864 | tf_op jit(solution)/shard_map/all_to_all | solution.py:378
  59.5 0.9 constant_dynamic-slice_fusion
  60.4 3.1 %collective-permute-start.13 = (bf16[256,256]{1,0:T(8,128)(2,1)S(1)}, bf16[256,256]{1,0:T(8,128)(2,1)S(1)}, u32[]{:S(2)}, u32[]{:S(2)}) collective-permute-start(bf16[256,256]{1,0:T(8,128)(2,1)S(1)} %constant_dynamic-slice_fusion), channel_id=1, source_target_pairs={{3,0},{0,1},{1,2},{2,3},{7,4},{4,5},{5,6},{6,7},{11,8},{8,9},{9,10... | collective-permute-start | bytes 393224 | tf_op jit(solution)/shard_map/ppermute | solution.py:338
  63.5 4.2 %collective-permute-start.12 = (bf16[256,256]{1,0:T(8,128)(2,1)S(1)}, bf16[256,256]{1,0:T(8,128)(2,1)S(1)}, u32[]{:S(2)}, u32[]{:S(2)}) collective-permute-start(bf16[256,256]{1,0:T(8,128)(2,1)S(1)} %constant_dynamic-slice_fusion), channel_id=1, source_target_pairs={{2,0},{3,1},{0,2},{1,3},{6,4},{7,5},{4,6},{5,7},{10,8},{11,9},{8,1... | collective-permute-start | bytes 393224 | tf_op jit(solution)/shard_map/ppermute | solution.py:338
  67.7 2.4 collective-permute-start.11
  70.1 9.2 %collective-permute-done.13 = bf16[256,256]{1,0:T(8,128)(2,1)S(1)} collective-permute-done((bf16[256,256]{1,0:T(8,128)(2,1)S(1)}, bf16[256,256]{1,0:T(8,128)(2,1)S(1)}, u32[]{:S(2)}, u32[]{:S(2)}) %collective-permute-start.13) | collective-permute-done | bytes 131104 | tf_op jit(solution)/shard_map/ppermute | solution.py:338
  79.3 3.8 %collective-permute-done.12 = bf16[256,256]{1,0:T(8,128)(2,1)S(1)} collective-permute-done((bf16[256,256]{1,0:T(8,128)(2,1)S(1)}, bf16[256,256]{1,0:T(8,128)(2,1)S(1)}, u32[]{:S(2)}, u32[]{:S(2)}) %collective-permute-start.12) | collective-permute-done | bytes 131104 | tf_op jit(solution)/shard_map/ppermute | solution.py:338
  83.1 2.1 collective-permute-start.16
  85.2 1.7 collective-permute-start.15
  86.8 0.8 collective-permute-start.14
  87.7 0.9 copy-done.1
  88.5 2.7 merge.1.v0
  91.2 1.9 collective-permute-done.16
  93.1 9.2 %collective-permute-done.15 = bf16[3,256,256]{2,1,0:T(8,128)(2,1)S(1)} collective-permute-done((bf16[3,256,256]{2,1,0:T(8,128)(2,1)S(1)}, bf16[3,256,256]{2,1,0:T(8,128)(2,1)S(1)}, u32[]{:S(2)}, u32[]{:S(2)}) %collective-permute-start.15) | collective-permute-done | bytes 393248 | tf_op jit(solution)/shard_map/ppermute | solution.py:339
  102.4 1.2 collective-permute-done.14
  103.7 1.8 collective-permute-start.17
  105.6 3.9 %collective-permute-start.10 = (bf16[128,256]{1,0:T(8,128)(2,1)S(1)}, bf16[128,256]{1,0:T(8,128)(2,1)S(1)}, u32[]{:S(2)}, u32[]{:S(2)}) collective-permute-start(bf16[128,256]{1,0:T(8,128)(2,1)S(1)} %copy-done.9), channel_id=1, source_target_pairs={{3,0},{0,1},{1,2},{2,3},{7,4},{4,5},{5,6},{6,7},{11,8},{8,9},{9,10... | collective-permute-start | bytes 196616 | tf_op jit(solution)/shard_map/ppermute | solution.py:388
  109.5 1.2 collective-permute-start.9
  110.6 2.1 collective-permute-start.8
  112.8 1.9 slots.1
  114.7 4.5 %collective-permute-done.9.v2 = bf16[128,256]{1,0:T(8,128)(2,1)S(1)} collective-permute-done((bf16[128,256]{1,0:T(8,128)(2,1)S(1)}, bf16[128,256]{1,0:T(8,128)(2,1)S(1)}, u32[]{:S(2)}, u32[]{:S(2)}) %collective-permute-start.9) | collective-permute-done | bytes 65568 | tf_op jit(solution)/shard_map/ppermute | solution.py:388
  119.2 0.6 copy-done.18
  119.8 0.0 copy-done.19
  119.8 0.6 copy-done.4
  120.3 7.1 %dispatch.1 = (bf16[1024,2048]{1,0:T(8,128)(2,1)}, bf16[128,512]{1,0:T(8,128)(2,1)}) custom-call(bf16[128,256]{1,0:T(8,128)(2,1)} %merge.1.v0, bf16[128,256]{1,0:T(8,128)(2,1)} %copy-done.19, bf16[128,256]{1,0:T(8,128)(2,1)} %copy-done.18, bf16[128,256]{1,0:T(8,128)(2,1)} %copy-done.17, bf16[128,2048]{1,0:T(8,128)(2,1)} %hid_ref.3, ...), custom_call_target="tpu_custom_call" | custom-call | tf_op jit(solution)/shard_map/dispatch/pallas_call | solution.py:397
  127.4 7.9 %all-to-all-start.2 = ((bf16[64,16,2048]{2,1,0:T(8,128)(2,1)}), bf16[64,16,2048]{2,1,0:T(8,128)(2,1)}, u32[]{:S(2)}, u32[]{:S(2)}) async-start(bf16[64,16,2048]{2,1,0:T(8,128)(2,1)} %bitcast.26), calls=%async_computation.2 | async-start | bytes 8388608 | tf_op jit(solution)/shard_map/all_to_all | solution.py:409
  135.3 0.9 copy.23
  136.2 1.9 copy.24
  138.1 0.1 broadcast_in_dim.3
  138.2 3.1 %pad_maximum_fusion.wgu_ref = bf16[2048,768]{1,0:T(8,128)(2,1)} fusion(bf16[2048,32]{1,0:T(8,128)(2,1)S(1)} %broadcast_in_dim.3, bf16[2048,352]{1,0:T(8,128)(2,1)S(1)} %bitcast.25, bf16[2048,352]{1,0:T(8,128)(2,1)S(1)} %bitcast.24), kind=kLoop, calls=%fused_computation | loop fusion | flops 12582912 | bytes 6160384 | tf_op jit(solution)/shard_map/concatenate | solution.py:412
  141.3 48.1 %all-to-all-done.2 = bf16[64,16,2048]{2,1,0:T(8,128)(2,1)} async-done(((bf16[64,16,2048]{2,1,0:T(8,128)(2,1)}), bf16[64,16,2048]{2,1,0:T(8,128)(2,1)}, u32[]{:S(2)}, u32[]{:S(2)}) %all-to-all-start.2) | async-done | bytes 4194336 | tf_op jit(solution)/shard_map/all_to_all | solution.py:409
  189.4 12.3 %expert.1 = bf16[1024,2048]{1,0:T(8,128)(2,1)} custom-call(bf16[1024,2048]{1,0:T(8,128)(2,1)} %bitcast.15.x_ref, bf16[2048,768]{1,0:T(8,128)(2,1)} %pad_maximum_fusion.wgu_ref, bf16[352,2048]{1,0:T(8,128)(2,1)} %bitcast.28), custom_call_target="tpu_custom_call" | custom-call | tf_op jit(solution)/shard_map/expert/pallas_call | solution.py:413
  201.7 5.9 %all-to-all-start.3 = ((bf16[64,16,2048]{2,1,0:T(8,128)(2,1)}), bf16[64,16,2048]{2,1,0:T(8,128)(2,1)}, u32[]{:S(2)}, u32[]{:S(2)}) async-start(bf16[64,16,2048]{2,1,0:T(8,128)(2,1)} %bitcast.23), calls=%async_computation.3 | async-start | bytes 8388608 | tf_op jit(solution)/shard_map/all_to_all | solution.py:422
  207.7 54.1 %all-to-all-done.3 = bf16[64,16,2048]{2,1,0:T(8,128)(2,1)} async-done(((bf16[64,16,2048]{2,1,0:T(8,128)(2,1)}), bf16[64,16,2048]{2,1,0:T(8,128)(2,1)}, u32[]{:S(2)}, u32[]{:S(2)}) %all-to-all-start.3) | async-done | bytes 4194336 | tf_op jit(solution)/shard_map/all_to_all | solution.py:422
  261.7 2.5 combine.7
  264.2 2.5 combine.6
  266.7 2.5 combine.5
  269.2 2.4 collective-permute-start.18
  271.6 1.5 collective-permute-start.19
  273.2 2.6 collective-permute-start.20
  275.8 0.6 dynamic-slice_bitcast_fusion
  276.4 2.5 combine.4.a_ref
  278.9 1.6 collective-permute-done.18.b_ref
  280.5 2.0 collective-permute-done.19.c_ref
  282.5 3.9 %collective-permute-done.20.d_ref = bf16[128,512]{1,0:T(8,128)(2,1)S(1)} collective-permute-done((bf16[128,512]{1,0:T(8,128)(2,1)S(1)}, bf16[128,512]{1,0:T(8,128)(2,1)S(1)}, u32[]{:S(2)}, u32[]{:S(2)}) %collective-permute-start.20) | collective-permute-done | bytes 131104 | tf_op jit(solution)/shard_map/ppermute | solution.py:445
  286.4 0.6 copy-done.16
  287.0 1.9 finish.1
  (53 shorter events, 0.4 us)
Async XLA Ops:
  5.1 6.5 %copy-start.11 = (bf16[1,128,576]{1,2,0:T(8,128)(2,1)S(1)}, bf16[1,128,576]{1,2,0:T(8,128)(2,1)}, u32[]{:S(2)}) copy-start(bf16[1,128,576]{1,2,0:T(8,128)(2,1)} %param.33) | copy-start | bytes 442372
  5.1 11.4 %copy-start.10 = (bf16[576,128]{1,0:T(8,128)(2,1)S(1)}, bf16[576,128]{1,0:T(8,128)(2,1)}, u32[]{:S(2)}) copy-start(bf16[576,128]{1,0:T(8,128)(2,1)} %get-tuple-element.14) | copy-start | bytes 442372
  5.1 26.4 %all-to-all-start = ((bf16[8,128,384]{2,1,0:T(8,128)(2,1)}), bf16[8,128,384]{2,1,0:T(8,128)(2,1)S(1)}, u32[]{:S(2)}, u32[]{:S(2)}) async-start(bf16[8,128,384]{2,1,0:T(8,128)(2,1)} %get-tuple-element.13), calls=%async_computation | async-start | bytes 1572864 | tf_op jit(solution)/shard_map/all_to_all | solution.py:333
  11.6 7.6 %collective-permute-start.2 = (bf16[576,128]{1,0:T(8,128)(2,1)S(1)}, bf16[576,128]{1,0:T(8,128)(2,1)S(1)}, u32[]{:S(2)}, u32[]{:S(2)}) collective-permute-start(bf16[576,128]{1,0:T(8,128)(2,1)S(1)} %bitcast.29), channel_id=1, source_target_pairs={{192,0},{196,4},{200,8},{204,12},{208,16},{212,20},{216,24},{220,2... | collective-permute-start | bytes 442376 | tf_op jit(solution)/shard_map/ppermute | solution.py:310
  12.9 8.6 %collective-permute-start.1 = (bf16[576,128]{1,0:T(8,128)(2,1)S(1)}, bf16[576,128]{1,0:T(8,128)(2,1)S(1)}, u32[]{:S(2)}, u32[]{:S(2)}) collective-permute-start(bf16[576,128]{1,0:T(8,128)(2,1)S(1)} %bitcast.30), channel_id=1, source_target_pairs={{128,0},{132,4},{136,8},{140,12},{144,16},{148,20},{152,24},{156,2... | collective-permute-start | bytes 442376 | tf_op jit(solution)/shard_map/ppermute | solution.py:310
  15.3 6.1 %collective-permute-start = (bf16[576,128]{1,0:T(8,128)(2,1)S(1)}, bf16[576,128]{1,0:T(8,128)(2,1)S(1)}, u32[]{:S(2)}, u32[]{:S(2)}) collective-permute-start(bf16[576,128]{1,0:T(8,128)(2,1)S(1)} %bitcast.31), channel_id=1, source_target_pairs={{64,0},{68,4},{72,8},{76,12},{80,16},{84,20},{88,24},{92,28},{96,3... | collective-permute-start | bytes 442376 | tf_op jit(solution)/shard_map/ppermute | solution.py:310
  16.5 11.3 %collective-permute-start.6 = (bf16[576,128]{1,0:T(8,128)(2,1)S(1)}, bf16[576,128]{1,0:T(8,128)(2,1)S(1)}, u32[]{:S(2)}, u32[]{:S(2)}) collective-permute-start(bf16[576,128]{1,0:T(8,128)(2,1)S(1)} %copy-done.10), channel_id=1, source_target_pairs={{192,0},{196,4},{200,8},{204,12},{208,16},{212,20},{216,24},{220,2... | collective-permute-start | bytes 442376 | tf_op jit(solution)/shard_map/ppermute | solution.py:310
  16.8 8.1 %collective-permute-start.4 = (bf16[576,128]{1,0:T(8,128)(2,1)S(1)}, bf16[576,128]{1,0:T(8,128)(2,1)S(1)}, u32[]{:S(2)}, u32[]{:S(2)}) collective-permute-start(bf16[576,128]{1,0:T(8,128)(2,1)S(1)} %copy-done.10), channel_id=1, source_target_pairs={{64,0},{68,4},{72,8},{76,12},{80,16},{84,20},{88,24},{92,28},{96,3... | collective-permute-start | bytes 442376 | tf_op jit(solution)/shard_map/ppermute | solution.py:310
  19.2 8.6 %collective-permute-start.5 = (bf16[576,128]{1,0:T(8,128)(2,1)S(1)}, bf16[576,128]{1,0:T(8,128)(2,1)S(1)}, u32[]{:S(2)}, u32[]{:S(2)}) collective-permute-start(bf16[576,128]{1,0:T(8,128)(2,1)S(1)} %copy-done.10), channel_id=1, source_target_pairs={{128,0},{132,4},{136,8},{140,12},{144,16},{148,20},{152,24},{156,2... | collective-permute-start | bytes 442376 | tf_op jit(solution)/shard_map/ppermute | solution.py:310
  21.5 9.9 %copy-start.3 = (bf16[576,512]{1,0:T(8,128)(2,1)}, bf16[576,512]{1,0:T(8,128)(2,1)S(1)}, u32[]{:S(2)}) copy-start(bf16[576,512]{1,0:T(8,128)(2,1)S(1)} %pad_maximum_fusion.1.pa_ref) | copy-start | bytes 1769476
  21.6 8.2 %collective-permute-start.3 = (bf16[576,512]{1,0:T(8,128)(2,1)S(1)}, bf16[576,512]{1,0:T(8,128)(2,1)S(1)}, u32[]{:S(2)}, u32[]{:S(2)}) collective-permute-start(bf16[576,512]{1,0:T(8,128)(2,1)S(1)} %pad_maximum_fusion.1.pa_ref), channel_id=1, source_target_pairs={{4,0},{0,4},{12,8},{8,12},{20,16},{16,20},{28,24},{24,28},{36,32},... | collective-permute-start | bytes 1769480 | tf_op jit(solution)/shard_map/ppermute | solution.py:312
  27.9 3.6 %copy-start.6 = (bf16[576,512]{1,0:T(8,128)(2,1)}, bf16[576,512]{1,0:T(8,128)(2,1)S(1)}, u32[]{:S(2)}) copy-start(bf16[576,512]{1,0:T(8,128)(2,1)S(1)} %constant_dynamic-update-slice_fusion.la_ref) | copy-start | bytes 1769476
  27.9 3.5 %collective-permute-start.7 = (bf16[576,512]{1,0:T(8,128)(2,1)S(1)}, bf16[576,512]{1,0:T(8,128)(2,1)S(1)}, u32[]{:S(2)}, u32[]{:S(2)}) collective-permute-start(bf16[576,512]{1,0:T(8,128)(2,1)S(1)} %constant_dynamic-update-slice_fusion.la_ref), channel_id=1, source_target_pairs={{4,0},{0,4},{12,8},{8,12},{20,16},{16,20},{28,24},{24,28},{36,32},... | collective-permute-start | bytes 1769480 | tf_op jit(solution)/shard_map/ppermute | solution.py:312
  29.8 1.6 copy-start.7
  31.4 0.8 copy-start.8
  32.3 0.9 copy-start
  54.4 33.2 %all-to-all-start.1 = ((bf16[8,128,384]{2,1,0:T(8,128)(2,1)}), bf16[8,128,384]{2,1,0:T(8,128)(2,1)S(1)}, u32[]{:S(2)}, u32[]{:S(2)}) async-start(bf16[8,128,384]{2,1,0:T(8,128)(2,1)} %attend.1), calls=%async_computation.1 | async-start | bytes 1572864 | tf_op jit(solution)/shard_map/all_to_all | solution.py:378
  60.4 18.9 %collective-permute-start.13 = (bf16[256,256]{1,0:T(8,128)(2,1)S(1)}, bf16[256,256]{1,0:T(8,128)(2,1)S(1)}, u32[]{:S(2)}, u32[]{:S(2)}) collective-permute-start(bf16[256,256]{1,0:T(8,128)(2,1)S(1)} %constant_dynamic-slice_fusion), channel_id=1, source_target_pairs={{3,0},{0,1},{1,2},{2,3},{7,4},{4,5},{5,6},{6,7},{11,8},{8,9},{9,10... | collective-permute-start | bytes 393224 | tf_op jit(solution)/shard_map/ppermute | solution.py:338
  63.5 19.6 %collective-permute-start.12 = (bf16[256,256]{1,0:T(8,128)(2,1)S(1)}, bf16[256,256]{1,0:T(8,128)(2,1)S(1)}, u32[]{:S(2)}, u32[]{:S(2)}) collective-permute-start(bf16[256,256]{1,0:T(8,128)(2,1)S(1)} %constant_dynamic-slice_fusion), channel_id=1, source_target_pairs={{2,0},{3,1},{0,2},{1,3},{6,4},{7,5},{4,6},{5,7},{10,8},{11,9},{8,1... | collective-permute-start | bytes 393224 | tf_op jit(solution)/shard_map/ppermute | solution.py:338
  67.7 15.4 %collective-permute-start.11 = (bf16[256,256]{1,0:T(8,128)(2,1)S(1)}, bf16[256,256]{1,0:T(8,128)(2,1)S(1)}, u32[]{:S(2)}, u32[]{:S(2)}) collective-permute-start(bf16[256,256]{1,0:T(8,128)(2,1)S(1)} %constant_dynamic-slice_fusion), channel_id=1, source_target_pairs={{1,0},{2,1},{3,2},{0,3},{5,4},{6,5},{7,6},{4,7},{9,8},{10,9},{11,1... | collective-permute-start | bytes 393224 | tf_op jit(solution)/shard_map/ppermute | solution.py:338
  83.1 10.0 %collective-permute-start.16 = (bf16[3,256,256]{2,1,0:T(8,128)(2,1)S(1)}, bf16[3,256,256]{2,1,0:T(8,128)(2,1)S(1)}, u32[]{:S(2)}, u32[]{:S(2)}) collective-permute-start(bf16[3,256,256]{2,1,0:T(8,128)(2,1)S(1)} %pad_maximum_fusion.2), channel_id=1, source_target_pairs={{192,0},{196,4},{200,8},{204,12},{208,16},{212,20},{216,24},{220,2... | collective-permute-start | bytes 1179656 | tf_op jit(solution)/shard_map/ppermute | solution.py:339
  85.2 17.2 %collective-permute-start.15 = (bf16[3,256,256]{2,1,0:T(8,128)(2,1)S(1)}, bf16[3,256,256]{2,1,0:T(8,128)(2,1)S(1)}, u32[]{:S(2)}, u32[]{:S(2)}) collective-permute-start(bf16[3,256,256]{2,1,0:T(8,128)(2,1)S(1)} %pad_maximum_fusion.2), channel_id=1, source_target_pairs={{128,0},{132,4},{136,8},{140,12},{144,16},{148,20},{152,24},{156,2... | collective-permute-start | bytes 1179656 | tf_op jit(solution)/shard_map/ppermute | solution.py:339
  86.8 16.8 %collective-permute-start.14 = (bf16[3,256,256]{2,1,0:T(8,128)(2,1)S(1)}, bf16[3,256,256]{2,1,0:T(8,128)(2,1)S(1)}, u32[]{:S(2)}, u32[]{:S(2)}) collective-permute-start(bf16[3,256,256]{2,1,0:T(8,128)(2,1)S(1)} %pad_maximum_fusion.2), channel_id=1, source_target_pairs={{64,0},{68,4},{72,8},{76,12},{80,16},{84,20},{88,24},{92,28},{96,3... | collective-permute-start | bytes 1179656 | tf_op jit(solution)/shard_map/ppermute | solution.py:339
  87.7 0.9 copy-start.1
  91.2 14.4 %copy-start.9 = (bf16[128,256]{1,0:T(8,128)(2,1)S(1)}, bf16[128,256]{1,0:T(8,128)(2,1)}, u32[]{:S(2)}) copy-start(bf16[128,256]{1,0:T(8,128)(2,1)} %merge.1.v0) | copy-start | bytes 196612
  103.7 15.4 %copy-start.2 = (bf16[12,256,256]{2,1,0:T(8,128)(2,1)}, bf16[12,256,256]{2,1,0:T(8,128)(2,1)S(1)}, u32[]{:S(2)}) copy-start(bf16[12,256,256]{2,1,0:T(8,128)(2,1)S(1)} %constant_dynamic-update-slice_fusion.4.wa_ref) | copy-start | bytes 4718596
  103.7 15.4 %collective-permute-start.17 = (bf16[12,256,256]{2,1,0:T(8,128)(2,1)S(1)}, bf16[12,256,256]{2,1,0:T(8,128)(2,1)S(1)}, u32[]{:S(2)}, u32[]{:S(2)}) collective-permute-start(bf16[12,256,256]{2,1,0:T(8,128)(2,1)S(1)} %constant_dynamic-update-slice_fusion.4.wa_ref), channel_id=1, source_target_pairs={{4,0},{0,4},{12,8},{8,12},{20,16},{16,20},{28,24},{24,28},{36,32},... | collective-permute-start | bytes 4718600 | tf_op jit(solution)/shard_map/ppermute | solution.py:392
  105.6 9.1 %collective-permute-start.10 = (bf16[128,256]{1,0:T(8,128)(2,1)S(1)}, bf16[128,256]{1,0:T(8,128)(2,1)S(1)}, u32[]{:S(2)}, u32[]{:S(2)}) collective-permute-start(bf16[128,256]{1,0:T(8,128)(2,1)S(1)} %copy-done.9), channel_id=1, source_target_pairs={{3,0},{0,1},{1,2},{2,3},{7,4},{4,5},{5,6},{6,7},{11,8},{8,9},{9,10... | collective-permute-start | bytes 196616 | tf_op jit(solution)/shard_map/ppermute | solution.py:388
  109.5 9.7 %collective-permute-start.9 = (bf16[128,256]{1,0:T(8,128)(2,1)S(1)}, bf16[128,256]{1,0:T(8,128)(2,1)S(1)}, u32[]{:S(2)}, u32[]{:S(2)}) collective-permute-start(bf16[128,256]{1,0:T(8,128)(2,1)S(1)} %copy-done.9), channel_id=1, source_target_pairs={{2,0},{3,1},{0,2},{1,3},{6,4},{7,5},{4,6},{5,7},{10,8},{11,9},{8,1... | collective-permute-start | bytes 196616 | tf_op jit(solution)/shard_map/ppermute | solution.py:388
  110.6 8.5 %collective-permute-start.8 = (bf16[128,256]{1,0:T(8,128)(2,1)S(1)}, bf16[128,256]{1,0:T(8,128)(2,1)S(1)}, u32[]{:S(2)}, u32[]{:S(2)}) collective-permute-start(bf16[128,256]{1,0:T(8,128)(2,1)S(1)} %copy-done.9), channel_id=1, source_target_pairs={{1,0},{2,1},{3,2},{0,3},{5,4},{6,5},{7,6},{4,7},{9,8},{10,9},{11,1... | collective-permute-start | bytes 196616 | tf_op jit(solution)/shard_map/ppermute | solution.py:388
  114.7 4.5 %copy-start.17 = (bf16[128,256]{1,0:T(8,128)(2,1)}, bf16[128,256]{1,0:T(8,128)(2,1)S(1)}, u32[]{:S(2)}) copy-start(bf16[128,256]{1,0:T(8,128)(2,1)S(1)} %collective-permute-done.10.v3) | copy-start | bytes 196612
  119.1 0.6 copy-start.18
  119.1 0.6 copy-start.19
  119.2 1.2 copy-start.4
  127.4 7.9 %copy-start.5 = (bf16[1,2048,352]{1,2,0:T(8,128)(2,1)S(1)}, bf16[1,2048,352]{1,2,0:T(8,128)(2,1)}, u32[]{:S(2)}) copy-start(bf16[1,2048,352]{1,2,0:T(8,128)(2,1)} %param.30) | copy-start | bytes 4325380
  127.4 62.0 %all-to-all-start.2 = ((bf16[64,16,2048]{2,1,0:T(8,128)(2,1)}), bf16[64,16,2048]{2,1,0:T(8,128)(2,1)}, u32[]{:S(2)}, u32[]{:S(2)}) async-start(bf16[64,16,2048]{2,1,0:T(8,128)(2,1)} %bitcast.26), calls=%async_computation.2 | async-start | bytes 8388608 | tf_op jit(solution)/shard_map/all_to_all | solution.py:409
  201.7 60.0 %all-to-all-start.3 = ((bf16[64,16,2048]{2,1,0:T(8,128)(2,1)}), bf16[64,16,2048]{2,1,0:T(8,128)(2,1)}, u32[]{:S(2)}, u32[]{:S(2)}) async-start(bf16[64,16,2048]{2,1,0:T(8,128)(2,1)} %bitcast.23), calls=%async_computation.3 | async-start | bytes 8388608 | tf_op jit(solution)/shard_map/all_to_all | solution.py:422
  266.7 5.0 %copy-start.13 = (bf16[128,512]{1,0:T(8,128)(2,1)S(1)}, bf16[128,512]{1,0:T(8,128)(2,1)}, u32[]{:S(2)}) copy-start(bf16[128,512]{1,0:T(8,128)(2,1)} %combine.6) | copy-start | bytes 393220
  266.7 6.5 %copy-start.12 = (bf16[128,512]{1,0:T(8,128)(2,1)S(1)}, bf16[128,512]{1,0:T(8,128)(2,1)}, u32[]{:S(2)}) copy-start(bf16[128,512]{1,0:T(8,128)(2,1)} %combine.7) | copy-start | bytes 393220
  269.2 11.3 %collective-permute-start.18 = (bf16[128,512]{1,0:T(8,128)(2,1)}, bf16[128,512]{1,0:T(8,128)(2,1)S(1)}, u32[]{:S(2)}, u32[]{:S(2)}) collective-permute-start(bf16[128,512]{1,0:T(8,128)(2,1)} %combine.5), channel_id=1, source_target_pairs={{3,0},{0,1},{1,2},{2,3},{7,4},{4,5},{5,6},{6,7},{11,8},{8,9},{9,10... | collective-permute-start | bytes 393224 | tf_op jit(solution)/shard_map/ppermute | solution.py:445
  271.6 10.9 %collective-permute-start.19 = (bf16[128,512]{1,0:T(8,128)(2,1)S(1)}, bf16[128,512]{1,0:T(8,128)(2,1)S(1)}, u32[]{:S(2)}, u32[]{:S(2)}) collective-permute-start(bf16[128,512]{1,0:T(8,128)(2,1)S(1)} %copy-done.13), channel_id=1, source_target_pairs={{2,0},{3,1},{0,2},{1,3},{6,4},{7,5},{4,6},{5,7},{10,8},{11,9},{8,1... | collective-permute-start | bytes 393224 | tf_op jit(solution)/shard_map/ppermute | solution.py:445
  273.2 13.2 %collective-permute-start.20 = (bf16[128,512]{1,0:T(8,128)(2,1)S(1)}, bf16[128,512]{1,0:T(8,128)(2,1)S(1)}, u32[]{:S(2)}, u32[]{:S(2)}) collective-permute-start(bf16[128,512]{1,0:T(8,128)(2,1)S(1)} %copy-done.12), channel_id=1, source_target_pairs={{1,0},{2,1},{3,2},{0,3},{5,4},{6,5},{7,6},{4,7},{9,8},{10,9},{11,1... | collective-permute-start | bytes 393224 | tf_op jit(solution)/shard_map/ppermute | solution.py:445
  280.5 5.9 %copy-start.14 = (bf16[128,512]{1,0:T(8,128)(2,1)}, bf16[128,512]{1,0:T(8,128)(2,1)S(1)}, u32[]{:S(2)}) copy-start(bf16[128,512]{1,0:T(8,128)(2,1)S(1)} %collective-permute-done.18.b_ref) | copy-start | bytes 393220
  282.5 3.9 %copy-start.15 = (bf16[128,512]{1,0:T(8,128)(2,1)}, bf16[128,512]{1,0:T(8,128)(2,1)S(1)}, u32[]{:S(2)}) copy-start(bf16[128,512]{1,0:T(8,128)(2,1)S(1)} %collective-permute-done.19.c_ref) | copy-start | bytes 393220
  286.4 0.6 copy-start.16

commit v2 on v1

--- a/solution.py
+++ b/solution.py
@@ -15,6 +15,7 @@
 LATENT = 512
 KEY = LATENT + ROPE
 SLOTS = 16
+STATS = 16
 EPSILON = 1e-06
 ROPE_BASE = 50000.0
 MASKED = -1e30
@@ -192,28 +193,31 @@
     stat = jnp.zeros((n, 128), F32)
     for h in range(2):
         rows = slice(h * n, (h + 1) * n)
-        out_ref[0, :, h * VDIM : (h + 1) * VDIM] = dot(
+        out_ref[0, :n, h * VDIM : (h + 1) * VDIM] = dot(
             att[rows], vu_ref[:, h * VDIM : (h + 1) * VDIM]
         ).astype(BF)
         for i, term in enumerate((hi, mid, low)):
             stat = jnp.where(lane == 3 * h + i, term[rows], stat)
-    out_ref[0, :, 2 * VDIM :] = stat.astype(BF)
+    out_ref[0, n:, :VDIM] = stat.T[:STATS].astype(BF)
+    out_ref[0, n:, VDIM:] = jnp.zeros((STATS, VDIM), BF)
 
 
 def merge_kernel(got_ref, out_ref):
     m = got_ref.shape[0]
+    n = out_ref.shape[0]
+    stats = jnp.concatenate([got_ref[i, n:, :VDIM] for i in range(m)], axis=0).astype(F32).T
     for h in range(2):
         lse = []
         for i in range(m):
-            st = got_ref[i, :, 2 * VDIM :].astype(F32)
-            lse.append(st[:, 3 * h : 3 * h + 1] + st[:, 3 * h + 1 : 3 * h + 2] + st[:, 3 * h + 2 : 3 * h + 3])
+            at = i * STATS + 3 * h
+            lse.append(stats[:, at : at + 1] + stats[:, at + 1 : at + 2] + stats[:, at + 2 : at + 3])
         top = functools.reduce(jnp.maximum, lse)
         den = jnp.zeros_like(top)
-        acc = jnp.zeros((got_ref.shape[1], VDIM), F32)
+        acc = jnp.zeros((n, VDIM), F32)
         for i in range(m):
             w = jnp.exp(lse[i] - top)
             den = den + w
-            acc = acc + w * got_ref[i, :, h * VDIM : (h + 1) * VDIM].astype(F32)
+            acc = acc + w * got_ref[i, :n, h * VDIM : (h + 1) * VDIM].astype(F32)
         out_ref[:, h * VDIM : (h + 1) * VDIM] = (acc / den).astype(BF)
 
 
@@ -238,12 +242,16 @@
     ghi = gate.astype(BF).astype(F32)
     glo = gate - ghi
     level = lax.broadcasted_iota(jnp.int32, (SLOTS, n), 0).astype(F32)
-    for e in range(experts):
-        hit = slot[e : e + 1, :] == level
-        rows = slice(e * SLOTS, (e + 1) * SLOTS)
-        oh_ref[rows, :] = jnp.where(hit, 1.0, 0.0).astype(BF)
-        hi_ref[rows, :] = jnp.where(hit, ghi[e : e + 1, :], 0.0).astype(BF)
-        lo_ref[rows, :] = jnp.where(hit, glo[e : e + 1, :], 0.0).astype(BF)
+    per = n // SLOTS
+    for first in range(0, experts, per):
+        parts = ([], [])
+        for e in range(first, first + per):
+            hit = slot[e : e + 1, :] == level
+            oh_ref[e * SLOTS : (e + 1) * SLOTS, :] = jnp.where(hit, 1.0, 0.0).astype(BF)
+            for part, v in zip(parts, (ghi, glo)):
+                part.append(jnp.where(hit, v[e : e + 1, :], 0.0))
+        for ref, part in zip((hi_ref, lo_ref), parts):
+            ref[:, first * SLOTS : (first + per) * SLOTS] = jnp.concatenate(part, axis=0).T.astype(BF)
 
 
 def dispatch_kernel(v0, v1, v2, v3, hid_ref, wo_ref, wa_ref, wb_ref, gain_ref, oh_ref, out_ref, mix_ref, in_ref, acc_ref):
@@ -282,8 +290,8 @@
 
 
 def combine_kernel(place, rows_ref, hi_ref, lo_ref, out_ref):
-    tn = (((0,), (0,)), ((), ()))
-    out_ref[...] = (dot(hi_ref[...], rows_ref[...], tn) + dot(lo_ref[...], rows_ref[...], tn)).astype(BF)
+    rows = rows_ref[...]
+    out_ref[...] = (dot(hi_ref[...], rows) + dot(lo_ref[...], rows)).astype(BF)
 
 
 def whole(n):
@@ -302,7 +310,7 @@
     quarter = d // tensor_count
     prefix = page_table.shape[1] * page_pool.shape[1]
     tok = token_order.reshape(seq_count, n)
-    params = pltpu.CompilerParams(vmem_limit_bytes=56 << 20)
+    params = pltpu.CompilerParams(vmem_limit_bytes=28 << 20)
 
     m = NZ * NY
 
@@ -340,7 +348,8 @@
 
     oh, ghi, glo = pl.pallas_call(
         slots_kernel,
-        out_shape=(jax.ShapeDtypeStruct((seq_count * SLOTS, n), BF),) * 3,
+        out_shape=(jax.ShapeDtypeStruct((seq_count * SLOTS, n), BF),)
+        + (jax.ShapeDtypeStruct((n, seq_count * SLOTS), BF),) * 2,
         in_specs=whole(2),
         out_specs=tuple(whole(3)),
         compiler_params=params,
@@ -354,7 +363,7 @@
 
     partial = pl.pallas_call(
         attend_kernel,
-        out_shape=jax.ShapeDtypeStruct((m, n, 3 * VDIM), BF),
+        out_shape=jax.ShapeDtypeStruct((m, n + STATS, 2 * VDIM), BF),
         grid_spec=pltpu.PrefetchScalarGridSpec(
             num_scalar_prefetch=3,
             grid=(m,),
@@ -362,7 +371,7 @@
             + [pl.BlockSpec((1,) + query.shape[1:], lambda j, *_: (j, 0, 0))]
             + [fixed((KEY, keys))] * 4
             + [fixed(w_key_up.shape), fixed(w_value_up.shape)],
-            out_specs=pl.BlockSpec((1, n, 3 * VDIM), lambda j, *_: (j, 0, 0)),
+            out_specs=pl.BlockSpec((1, n + STATS, 2 * VDIM), lambda j, *_: (j, 0, 0)),
             scratch_shapes=[
                 pltpu.VMEM((2 * n, 4 * keys), F32),
                 pltpu.VMEM((2 * n, KEY), BF),

time: 290 us -> 289 us (level)
  Pallas kernels: 61.5 us -> 43.9 us
  local copies, waits for them, and re-layouts: 8.98 us -> 24.8 us
    unnamed x48 -> x74, local copies, waits for them, and re-layouts: 7.32 us -> 23.3 us
    pallas_call x1, Pallas kernels: 7.06 us -> 2.8 us  [local(): pl.pallas_call(dispatch_kernel, out_shape=(jax.ShapeDtypeStruct((rows, d)...]
    pallas_call x4, Pallas kernels: 9.95 us -> 6.68 us  [combined(): pl.pallas_call(combine_kernel, out_shape=piece, grid_spec=pltpu.PrefetchS...]
  transfers between devices with their start and end apart: 25 -> 25, of which waited for: 14 -> 13; matrix products, arithmetic and copies ran while one was open for 3% -> 3% of each run, Pallas kernels for 2% -> 1%
where the time goes in v2:
time: 289 us; the launch traced here: 288 us
  waiting for transfers between devices  145 us (50%)
  starting transfers between devices  69.5 us (24%)
  Pallas kernels  43.9 us (15%)
  local copies, waits for them, and re-layouts  24.8 us (9%)
  other arithmetic  3.46 us (1%)
    all_to_all x1, waiting for transfers between devices, local(): lax.all_to_all(results.reshape(seq_count, SLOTS, d), 'seq', 0, 0, tiled=T...  54.1 us
    all_to_all x1, waiting for transfers between devices, local(): lax.all_to_all(outbound.reshape(seq_count, SLOTS, d), 'seq', 0, 0, tiled=...  47.5 us
    unnamed x74, local copies, waits for them, and re-layouts  23.3 us
    pallas_call x1, Pallas kernels, local(): pl.pallas_call(attend_kernel, out_shape=jax.ShapeDtypeStruct((m, n + STAT...  19.5 us
    ppermute x3, waiting for transfers between devices, local(): lax.ppermute(other, 'seq', seq_perm(i, 0, 0, 0))  14.7 us
    ppermute x3, waiting for transfers between devices, local(): lax.ppermute(mine, 'tensor', tensor_from(j, tensor_count))  11.7 us
    pallas_call x1, Pallas kernels, local(): pl.pallas_call(expert_kernel, out_shape=jax.ShapeDtypeStruct((rows, d), B...  9.85 us
    ppermute x3, starting transfers between devices, local(): lax.ppermute(mine, 'tensor', tensor_from(j, tensor_count))  9.67 us
  transfers between devices with their start and end apart: 25, of which 13 were waited for; matrix products, arithmetic and copies ran while one was open for 3% of the time, Pallas kernels for 1%

profile of v2, /device:TPU:1, one launch (start us, length us, event | category | flops | bytes accessed | tf_op | source)
XLA Modules:
  0.0 288.0 jit_solution(7797723700258205912)
XLA Ops:
  0.6 1.7 copy-done.4
  2.3 1.0 copy-done.5
  3.3 1.4 copy-done.7
  4.8 0.8 copy-done.17
  5.5 0.7 copy-done.19
  8.9 2.7 project.1
  11.6 6.5 %all-to-all-start = ((bf16[8,128,384]{2,1,0:T(8,128)(2,1)}), bf16[8,128,384]{2,1,0:T(8,128)(2,1)S(1)}, u32[]{:S(2)}, u32[]{:S(2)}) async-start(bf16[8,128,384]{2,1,0:T(8,128)(2,1)} %get-tuple-element.13), calls=%async_computation | async-start | bytes 1572864 | tf_op jit(solution)/shard_map/all_to_all | solution.py:341
  18.2 1.3 collective-permute-start.2
  19.5 2.4 collective-permute-start.1
  21.9 1.2 collective-permute-start
  23.4 2.4 collective-permute-start.4
  25.9 2.2 collective-permute-done.1
  28.1 3.3 %collective-permute-start.3 = (bf16[576,512]{1,0:T(8,128)(2,1)S(1)}, bf16[576,512]{1,0:T(8,128)(2,1)S(1)}, u32[]{:S(2)}, u32[]{:S(2)}) collective-permute-start(bf16[576,512]{1,0:T(8,128)(2,1)S(1)} %pad_maximum_fusion.1.pa_ref), channel_id=1, source_target_pairs={{4,0},{0,4},{12,8},{8,12},{20,16},{16,20},{28,24},{24,28},{36,32},... | collective-permute-start | bytes 1769480 | tf_op jit(solution)/shard_map/ppermute | solution.py:320
  31.5 2.9 collective-permute-done.5
  34.5 1.9 collective-permute-start.7
  36.4 0.8 copy-done.10
  37.2 0.8 collective-permute-done.7.lb_ref
  38.0 0.8 copy-done.12
  38.9 1.1 copy-done.11
  39.9 1.1 copy-done.13
  41.0 0.8 copy-done.18
  41.8 19.5 %attend.1 = bf16[8,144,256]{2,1,0:T(8,128)(2,1)} custom-call(s32[16]{0:T(128)S(1)} %copy-done.27, s32[16]{0:T(128)S(1)} %copy-done.28, s32[4,16]{1,0:T(4,128)S(1)} %copy-done.25, s32[64,128]{1,0:T(8,128)S(1)} %bitcast.28, bf16[8,128,384]{2,1,0:T(8,128)(2,1)S(1)} %all-to-all-done.q_ref, bf16[576,512]{1,0:T(8,128)(2,1)S(1)} %pad_maximum_fusion.1.pa_ref, ...), custom_call_target="tpu_custom_call" | custom-call | tf_op jit(solution)/shard_map/attend/pallas_call | solution.py:364
  61.3 5.1 %all-to-all-start.1 = ((bf16[8,144,256]{2,1,0:T(8,128)(2,1)}), bf16[8,144,256]{2,1,0:T(8,128)(2,1)S(1)}, u32[]{:S(2)}, u32[]{:S(2)}) async-start(bf16[8,144,256]{2,1,0:T(8,128)(2,1)} %attend.1), calls=%async_computation.1 | async-start | bytes 1179648 | tf_op jit(solution)/shard_map/all_to_all | solution.py:387
  66.5 3.1 %collective-permute-start.13 = (bf16[256,256]{1,0:T(8,128)(2,1)S(1)}, bf16[256,256]{1,0:T(8,128)(2,1)S(1)}, u32[]{:S(2)}, u32[]{:S(2)}) collective-permute-start(bf16[256,256]{1,0:T(8,128)(2,1)S(1)} %constant_dynamic-slice_fusion), channel_id=1, source_target_pairs={{3,0},{0,1},{1,2},{2,3},{7,4},{4,5},{5,6},{6,7},{11,8},{8,9},{9,10... | collective-permute-start | bytes 393224 | tf_op jit(solution)/shard_map/ppermute | solution.py:346
  69.5 4.2 %collective-permute-start.12 = (bf16[256,256]{1,0:T(8,128)(2,1)S(1)}, bf16[256,256]{1,0:T(8,128)(2,1)S(1)}, u32[]{:S(2)}, u32[]{:S(2)}) collective-permute-start(bf16[256,256]{1,0:T(8,128)(2,1)S(1)} %constant_dynamic-slice_fusion), channel_id=1, source_target_pairs={{2,0},{3,1},{0,2},{1,3},{6,4},{7,5},{4,6},{5,7},{10,8},{11,9},{8,1... | collective-permute-start | bytes 393224 | tf_op jit(solution)/shard_map/ppermute | solution.py:346
  73.7 2.4 collective-permute-start.11
  76.1 8.0 %collective-permute-done.13 = bf16[256,256]{1,0:T(8,128)(2,1)S(1)} collective-permute-done((bf16[256,256]{1,0:T(8,128)(2,1)S(1)}, bf16[256,256]{1,0:T(8,128)(2,1)S(1)}, u32[]{:S(2)}, u32[]{:S(2)}) %collective-permute-start.13) | collective-permute-done | bytes 131104 | tf_op jit(solution)/shard_map/ppermute | solution.py:346
  84.1 3.7 %collective-permute-done.12 = bf16[256,256]{1,0:T(8,128)(2,1)S(1)} collective-permute-done((bf16[256,256]{1,0:T(8,128)(2,1)S(1)}, bf16[256,256]{1,0:T(8,128)(2,1)S(1)}, u32[]{:S(2)}, u32[]{:S(2)}) %collective-permute-start.12) | collective-permute-done | bytes 131104 | tf_op jit(solution)/shard_map/ppermute | solution.py:346
  87.9 2.0 collective-permute-start.16
  89.9 1.7 collective-permute-start.15
  91.6 0.8 collective-permute-start.14
  92.4 1.2 merge.1.v0
  93.7 4.2 %collective-permute-done.16 = bf16[3,256,256]{2,1,0:T(8,128)(2,1)S(1)} collective-permute-done((bf16[3,256,256]{2,1,0:T(8,128)(2,1)S(1)}, bf16[3,256,256]{2,1,0:T(8,128)(2,1)S(1)}, u32[]{:S(2)}, u32[]{:S(2)}) %collective-permute-start.16) | collective-permute-done | bytes 393248 | tf_op jit(solution)/shard_map/ppermute | solution.py:347
  97.9 9.2 %collective-permute-done.15 = bf16[3,256,256]{2,1,0:T(8,128)(2,1)S(1)} collective-permute-done((bf16[3,256,256]{2,1,0:T(8,128)(2,1)S(1)}, bf16[3,256,256]{2,1,0:T(8,128)(2,1)S(1)}, u32[]{:S(2)}, u32[]{:S(2)}) %collective-permute-start.15) | collective-permute-done | bytes 393248 | tf_op jit(solution)/shard_map/ppermute | solution.py:347
  107.1 1.3 collective-permute-done.14
  108.4 1.0 constant_dynamic-update-slice_fusion.6
  109.5 1.8 collective-permute-start.17
  111.3 4.0 %collective-permute-start.10 = (bf16[128,256]{1,0:T(8,128)(2,1)S(1)}, bf16[128,256]{1,0:T(8,128)(2,1)S(1)}, u32[]{:S(2)}, u32[]{:S(2)}) collective-permute-start(bf16[128,256]{1,0:T(8,128)(2,1)S(1)} %merge.1.v0), channel_id=1, source_target_pairs={{3,0},{0,1},{1,2},{2,3},{7,4},{4,5},{5,6},{6,7},{11,8},{8,9},{9,10... | collective-permute-start | bytes 196616 | tf_op jit(solution)/shard_map/ppermute | solution.py:397
  115.3 1.2 collective-permute-start.9
  116.4 2.1 collective-permute-start.8
  119.6 4.2 %collective-permute-done.9.v2 = bf16[128,256]{1,0:T(8,128)(2,1)S(1)} collective-permute-done((bf16[128,256]{1,0:T(8,128)(2,1)S(1)}, bf16[128,256]{1,0:T(8,128)(2,1)S(1)}, u32[]{:S(2)}, u32[]{:S(2)}) %collective-permute-start.9) | collective-permute-done | bytes 65568 | tf_op jit(solution)/shard_map/ppermute | solution.py:397
  123.9 2.8 dispatch.1
  126.7 2.0 copy-done.3
  128.7 8.8 %all-to-all-start.2 = ((bf16[64,16,2048]{2,1,0:T(8,128)(2,1)}), bf16[64,16,2048]{2,1,0:T(8,128)(2,1)}, u32[]{:S(2)}, u32[]{:S(2)}) async-start(bf16[64,16,2048]{2,1,0:T(8,128)(2,1)} %bitcast.24), calls=%async_computation.2 | async-start | bytes 8388608 | tf_op jit(solution)/shard_map/all_to_all | solution.py:418
  137.5 1.6 copy.23
  139.1 1.6 copy.24
  140.8 3.3 %pad_maximum_fusion.wgu_ref = bf16[2048,768]{1,0:T(8,128)(2,1)S(1)} fusion(bf16[2048,32]{1,0:T(8,128)(2,1)S(1)} %broadcast_in_dim.3, bf16[2048,352]{1,0:T(8,128)(2,1)} %bitcast.35, bf16[2048,352]{1,0:T(8,128)(2,1)} %bitcast.34), kind=kLoop, calls=%fused_computation | loop fusion | flops 12582912 | bytes 6160384 | tf_op jit(solution)/shard_map/concatenate | solution.py:421
  144.1 47.5 %all-to-all-done.2 = bf16[64,16,2048]{2,1,0:T(8,128)(2,1)} async-done(((bf16[64,16,2048]{2,1,0:T(8,128)(2,1)}), bf16[64,16,2048]{2,1,0:T(8,128)(2,1)}, u32[]{:S(2)}, u32[]{:S(2)}) %all-to-all-start.2) | async-done | bytes 4194336 | tf_op jit(solution)/shard_map/all_to_all | solution.py:418
  191.6 1.4 copy-done.8
  193.0 9.9 %expert.1 = bf16[1024,2048]{1,0:T(8,128)(2,1)S(1)} custom-call(bf16[1024,2048]{1,0:T(8,128)(2,1)} %bitcast.15.x_ref, bf16[2048,768]{1,0:T(8,128)(2,1)S(1)} %pad_maximum_fusion.wgu_ref, bf16[352,2048]{1,0:T(8,128)(2,1)S(1)} %bitcast.26), custom_call_target="tpu_custom_call" | custom-call | tf_op jit(solution)/shard_map/expert/pallas_call | solution.py:422
  202.8 2.0 copy-done
  204.8 6.1 %all-to-all-start.3 = ((bf16[64,16,2048]{2,1,0:T(8,128)(2,1)}), bf16[64,16,2048]{2,1,0:T(8,128)(2,1)}, u32[]{:S(2)}, u32[]{:S(2)}) async-start(bf16[64,16,2048]{2,1,0:T(8,128)(2,1)} %bitcast.23), calls=%async_computation.3 | async-start | bytes 8388608 | tf_op jit(solution)/shard_map/all_to_all | solution.py:431
  210.9 54.1 %all-to-all-done.3 = bf16[64,16,2048]{2,1,0:T(8,128)(2,1)} async-done(((bf16[64,16,2048]{2,1,0:T(8,128)(2,1)}), bf16[64,16,2048]{2,1,0:T(8,128)(2,1)}, u32[]{:S(2)}, u32[]{:S(2)}) %all-to-all-start.3) | async-done | bytes 4194336 | tf_op jit(solution)/shard_map/all_to_all | solution.py:431
  265.0 1.7 combine.7
  266.6 1.7 combine.6
  268.3 1.7 combine.5
  270.0 2.4 collective-permute-start.18
  272.5 1.7 collective-permute-start.19
  274.1 2.7 collective-permute-start.20
  276.9 1.4 dynamic-slice_bitcast_fusion
  278.2 1.7 combine.4.a_ref
  279.9 3.5 %collective-permute-done.19.c_ref = bf16[128,512]{1,0:T(8,128)(2,1)S(1)} collective-permute-done((bf16[128,512]{1,0:T(8,128)(2,1)S(1)}, bf16[128,512]{1,0:T(8,128)(2,1)S(1)}, u32[]{:S(2)}, u32[]{:S(2)}) %collective-permute-start.19) | collective-permute-done | bytes 131104 | tf_op jit(solution)/shard_map/ppermute | solution.py:454
  283.4 3.9 %collective-permute-done.20.d_ref = bf16[128,512]{1,0:T(8,128)(2,1)S(1)} collective-permute-done((bf16[128,512]{1,0:T(8,128)(2,1)S(1)}, bf16[128,512]{1,0:T(8,128)(2,1)S(1)}, u32[]{:S(2)}, u32[]{:S(2)}) %collective-permute-start.20) | collective-permute-done | bytes 131104 | tf_op jit(solution)/shard_map/ppermute | solution.py:454
  287.3 0.7 finish.1
  (79 shorter events, 4.7 us)
Async XLA Ops:
  0.6 1.7 copy-start.4
  2.3 1.0 copy-start.5
  3.3 1.4 copy-start.7
  4.7 0.8 copy-start.17
  5.5 0.7 copy-start.19
  6.2 0.7 copy-start.20
  6.9 0.7 copy-start.24
  7.6 0.7 copy-start.26
  8.3 0.7 copy-start.29
  11.6 19.9 %copy-start.16 = (bf16[576,128]{1,0:T(8,128)(2,1)}, bf16[576,128]{1,0:T(8,128)(2,1)S(1)}, u32[]{:S(2)}) copy-start(bf16[576,128]{1,0:T(8,128)(2,1)S(1)} %get-tuple-element.14) | copy-start | bytes 442372
  11.6 6.6 %copy-start.32 = (bf16[1,128,576]{1,2,0:T(8,128)(2,1)S(1)}, bf16[1,128,576]{1,2,0:T(8,128)(2,1)}, u32[]{:S(2)}) copy-start(bf16[1,128,576]{1,2,0:T(8,128)(2,1)} %param.33) | copy-start | bytes 442372
  11.6 27.2 %all-to-all-start = ((bf16[8,128,384]{2,1,0:T(8,128)(2,1)}), bf16[8,128,384]{2,1,0:T(8,128)(2,1)S(1)}, u32[]{:S(2)}, u32[]{:S(2)}) async-start(bf16[8,128,384]{2,1,0:T(8,128)(2,1)} %get-tuple-element.13), calls=%async_computation | async-start | bytes 1572864 | tf_op jit(solution)/shard_map/all_to_all | solution.py:341
  18.1 20.7 %copy-start.14 = (bf16[512,256]{1,0:T(8,128)(2,1)S(1)}, bf16[512,256]{1,0:T(8,128)(2,1)}, u32[]{:S(2)}) copy-start(bf16[512,256]{1,0:T(8,128)(2,1)} %ku_ref.1) | copy-start | bytes 786436
  18.1 20.7 %copy-start.15 = (bf16[512,256]{1,0:T(8,128)(2,1)S(1)}, bf16[512,256]{1,0:T(8,128)(2,1)}, u32[]{:S(2)}) copy-start(bf16[512,256]{1,0:T(8,128)(2,1)} %vu_ref.1) | copy-start | bytes 786436
  18.1 20.7 %copy-start.25 = (s32[4,16]{1,0:T(4,128)S(1)}, s32[4,16]{1,0:T(4,128)}, u32[]{:S(2)}) copy-start(s32[4,16]{1,0:T(4,128)} %table.1) | copy-start | bytes 772
  18.1 20.7 %copy-start.27 = (s32[16]{0:T(128)S(1)}, s32[16]{0:T(128)}, u32[]{:S(2)}) copy-start(s32[16]{0:T(128)} %lengths.3) | copy-start | bytes 196
  18.1 20.7 %copy-start.28 = (s32[16]{0:T(128)S(1)}, s32[16]{0:T(128)}, u32[]{:S(2)}) copy-start(s32[16]{0:T(128)} %group.1) | copy-start | bytes 196
  18.2 7.6 %collective-permute-start.2 = (bf16[576,128]{1,0:T(8,128)(2,1)S(1)}, bf16[576,128]{1,0:T(8,128)(2,1)S(1)}, u32[]{:S(2)}, u32[]{:S(2)}) collective-permute-start(bf16[576,128]{1,0:T(8,128)(2,1)S(1)} %bitcast.36), channel_id=1, source_target_pairs={{192,0},{196,4},{200,8},{204,12},{208,16},{212,20},{216,24},{220,2... | collective-permute-start | bytes 442376 | tf_op jit(solution)/shard_map/ppermute | solution.py:318
  19.5 8.6 %collective-permute-start.1 = (bf16[576,128]{1,0:T(8,128)(2,1)S(1)}, bf16[576,128]{1,0:T(8,128)(2,1)S(1)}, u32[]{:S(2)}, u32[]{:S(2)}) collective-permute-start(bf16[576,128]{1,0:T(8,128)(2,1)S(1)} %bitcast.37), channel_id=1, source_target_pairs={{128,0},{132,4},{136,8},{140,12},{144,16},{148,20},{152,24},{156,2... | collective-permute-start | bytes 442376 | tf_op jit(solution)/shard_map/ppermute | solution.py:318
  21.9 6.1 %collective-permute-start = (bf16[576,128]{1,0:T(8,128)(2,1)S(1)}, bf16[576,128]{1,0:T(8,128)(2,1)S(1)}, u32[]{:S(2)}, u32[]{:S(2)}) collective-permute-start(bf16[576,128]{1,0:T(8,128)(2,1)S(1)} %bitcast.38), channel_id=1, source_target_pairs={{64,0},{68,4},{72,8},{76,12},{80,16},{84,20},{88,24},{92,28},{96,3... | collective-permute-start | bytes 442376 | tf_op jit(solution)/shard_map/ppermute | solution.py:318
  23.1 11.3 %collective-permute-start.6 = (bf16[576,128]{1,0:T(8,128)(2,1)S(1)}, bf16[576,128]{1,0:T(8,128)(2,1)S(1)}, u32[]{:S(2)}, u32[]{:S(2)}) collective-permute-start(bf16[576,128]{1,0:T(8,128)(2,1)S(1)} %get-tuple-element.14), channel_id=1, source_target_pairs={{192,0},{196,4},{200,8},{204,12},{208,16},{212,20},{216,24},{220,2... | collective-permute-start | bytes 442376 | tf_op jit(solution)/shard_map/ppermute | solution.py:318
  23.4 8.1 %collective-permute-start.4 = (bf16[576,128]{1,0:T(8,128)(2,1)S(1)}, bf16[576,128]{1,0:T(8,128)(2,1)S(1)}, u32[]{:S(2)}, u32[]{:S(2)}) collective-permute-start(bf16[576,128]{1,0:T(8,128)(2,1)S(1)} %get-tuple-element.14), channel_id=1, source_target_pairs={{64,0},{68,4},{72,8},{76,12},{80,16},{84,20},{88,24},{92,28},{96,3... | collective-permute-start | bytes 442376 | tf_op jit(solution)/shard_map/ppermute | solution.py:318
  25.8 8.6 %collective-permute-start.5 = (bf16[576,128]{1,0:T(8,128)(2,1)S(1)}, bf16[576,128]{1,0:T(8,128)(2,1)S(1)}, u32[]{:S(2)}, u32[]{:S(2)}) collective-permute-start(bf16[576,128]{1,0:T(8,128)(2,1)S(1)} %get-tuple-element.14), channel_id=1, source_target_pairs={{128,0},{132,4},{136,8},{140,12},{144,16},{148,20},{152,24},{156,2... | collective-permute-start | bytes 442376 | tf_op jit(solution)/shard_map/ppermute | solution.py:318
  28.1 8.3 %collective-permute-start.3 = (bf16[576,512]{1,0:T(8,128)(2,1)S(1)}, bf16[576,512]{1,0:T(8,128)(2,1)S(1)}, u32[]{:S(2)}, u32[]{:S(2)}) collective-permute-start(bf16[576,512]{1,0:T(8,128)(2,1)S(1)} %pad_maximum_fusion.1.pa_ref), channel_id=1, source_target_pairs={{4,0},{0,4},{12,8},{8,12},{20,16},{16,20},{28,24},{24,28},{36,32},... | collective-permute-start | bytes 1769480 | tf_op jit(solution)/shard_map/ppermute | solution.py:320
  34.5 31.9 %copy-start.9 = (bf16[256,2048]{1,0:T(8,128)(2,1)S(1)}, bf16[256,2048]{1,0:T(8,128)(2,1)}, u32[]{:S(2)}) copy-start(bf16[256,2048]{1,0:T(8,128)(2,1)} %wo_ref.1) | copy-start | bytes 3145732
  34.5 3.5 %collective-permute-start.7 = (bf16[576,512]{1,0:T(8,128)(2,1)S(1)}, bf16[576,512]{1,0:T(8,128)(2,1)S(1)}, u32[]{:S(2)}, u32[]{:S(2)}) collective-permute-start(bf16[576,512]{1,0:T(8,128)(2,1)S(1)} %constant_dynamic-update-slice_fusion.la_ref), channel_id=1, source_target_pairs={{4,0},{0,4},{12,8},{8,12},{20,16},{16,20},{28,24},{24,28},{36,32},... | collective-permute-start | bytes 1769480 | tf_op jit(solution)/shard_map/ppermute | solution.py:320
  36.4 0.8 copy-start.10
  38.0 0.8 copy-start.12
  38.9 1.1 copy-start.11
  39.9 1.1 copy-start.13
  41.0 0.8 copy-start.18
  61.3 31.1 %all-to-all-start.1 = ((bf16[8,144,256]{2,1,0:T(8,128)(2,1)}), bf16[8,144,256]{2,1,0:T(8,128)(2,1)S(1)}, u32[]{:S(2)}, u32[]{:S(2)}) async-start(bf16[8,144,256]{2,1,0:T(8,128)(2,1)} %attend.1), calls=%async_computation.1 | async-start | bytes 1179648 | tf_op jit(solution)/shard_map/all_to_all | solution.py:387
  66.5 17.6 %collective-permute-start.13 = (bf16[256,256]{1,0:T(8,128)(2,1)S(1)}, bf16[256,256]{1,0:T(8,128)(2,1)S(1)}, u32[]{:S(2)}, u32[]{:S(2)}) collective-permute-start(bf16[256,256]{1,0:T(8,128)(2,1)S(1)} %constant_dynamic-slice_fusion), channel_id=1, source_target_pairs={{3,0},{0,1},{1,2},{2,3},{7,4},{4,5},{5,6},{6,7},{11,8},{8,9},{9,10... | collective-permute-start | bytes 393224 | tf_op jit(solution)/shard_map/ppermute | solution.py:346
  69.5 18.3 %collective-permute-start.12 = (bf16[256,256]{1,0:T(8,128)(2,1)S(1)}, bf16[256,256]{1,0:T(8,128)(2,1)S(1)}, u32[]{:S(2)}, u32[]{:S(2)}) collective-permute-start(bf16[256,256]{1,0:T(8,128)(2,1)S(1)} %constant_dynamic-slice_fusion), channel_id=1, source_target_pairs={{2,0},{3,1},{0,2},{1,3},{6,4},{7,5},{4,6},{5,7},{10,8},{11,9},{8,1... | collective-permute-start | bytes 393224 | tf_op jit(solution)/shard_map/ppermute | solution.py:346
  73.7 14.1 %collective-permute-start.11 = (bf16[256,256]{1,0:T(8,128)(2,1)S(1)}, bf16[256,256]{1,0:T(8,128)(2,1)S(1)}, u32[]{:S(2)}, u32[]{:S(2)}) collective-permute-start(bf16[256,256]{1,0:T(8,128)(2,1)S(1)} %constant_dynamic-slice_fusion), channel_id=1, source_target_pairs={{1,0},{2,1},{3,2},{0,3},{5,4},{6,5},{7,6},{4,7},{9,8},{10,9},{11,1... | collective-permute-start | bytes 393224 | tf_op jit(solution)/shard_map/ppermute | solution.py:346
  87.9 10.0 %collective-permute-start.16 = (bf16[3,256,256]{2,1,0:T(8,128)(2,1)S(1)}, bf16[3,256,256]{2,1,0:T(8,128)(2,1)S(1)}, u32[]{:S(2)}, u32[]{:S(2)}) collective-permute-start(bf16[3,256,256]{2,1,0:T(8,128)(2,1)S(1)} %pad_maximum_fusion.2), channel_id=1, source_target_pairs={{192,0},{196,4},{200,8},{204,12},{208,16},{212,20},{216,24},{220,2... | collective-permute-start | bytes 1179656 | tf_op jit(solution)/shard_map/ppermute | solution.py:347
  89.9 17.2 %collective-permute-start.15 = (bf16[3,256,256]{2,1,0:T(8,128)(2,1)S(1)}, bf16[3,256,256]{2,1,0:T(8,128)(2,1)S(1)}, u32[]{:S(2)}, u32[]{:S(2)}) collective-permute-start(bf16[3,256,256]{2,1,0:T(8,128)(2,1)S(1)} %pad_maximum_fusion.2), channel_id=1, source_target_pairs={{128,0},{132,4},{136,8},{140,12},{144,16},{148,20},{152,24},{156,2... | collective-permute-start | bytes 1179656 | tf_op jit(solution)/shard_map/ppermute | solution.py:347
  91.6 16.8 %collective-permute-start.14 = (bf16[3,256,256]{2,1,0:T(8,128)(2,1)S(1)}, bf16[3,256,256]{2,1,0:T(8,128)(2,1)}, u32[]{:S(2)}, u32[]{:S(2)}) collective-permute-start(bf16[3,256,256]{2,1,0:T(8,128)(2,1)S(1)} %pad_maximum_fusion.2), channel_id=1, source_target_pairs={{64,0},{68,4},{72,8},{76,12},{80,16},{84,20},{88,24},{92,28},{96,3... | collective-permute-start | bytes 1179656 | tf_op jit(solution)/shard_map/ppermute | solution.py:347
  93.6 24.9 %copy-start.22 = (s32[128,6]{0,1:T(8,128)S(1)}, s32[128,6]{0,1:T(8,128)}, u32[]{:S(2)}) copy-start(s32[128,6]{0,1:T(8,128)} %param.38) | copy-start | bytes 9220
  93.6 24.9 %copy-start.23 = (f32[128,6]{0,1:T(8,128)S(1)}, f32[128,6]{0,1:T(8,128)}, u32[]{:S(2)}) copy-start(f32[128,6]{0,1:T(8,128)} %param.39) | copy-start | bytes 9220
  93.6 30.3 %copy-start.6 = (bf16[128,2048]{1,0:T(8,128)(2,1)S(1)}, bf16[128,2048]{1,0:T(8,128)(2,1)}, u32[]{:S(2)}) copy-start(bf16[128,2048]{1,0:T(8,128)(2,1)} %hid_ref.3) | copy-start | bytes 1572868
  93.7 30.2 %copy-start.21 = (f32[2048]{0:T(1024)S(1)}, f32[2048]{0:T(1024)}, u32[]{:S(2)}) copy-start(f32[2048]{0:T(1024)} %param.29) | copy-start | bytes 24580
  109.5 14.4 %collective-permute-start.17 = (bf16[12,256,256]{2,1,0:T(8,128)(2,1)S(1)}, bf16[12,256,256]{2,1,0:T(8,128)(2,1)S(1)}, u32[]{:S(2)}, u32[]{:S(2)}) collective-permute-start(bf16[12,256,256]{2,1,0:T(8,128)(2,1)S(1)} %constant_dynamic-update-slice_fusion.4.wa_ref), channel_id=1, source_target_pairs={{4,0},{0,4},{12,8},{8,12},{20,16},{16,20},{28,24},{24,28},{36,32},... | collective-permute-start | bytes 4718600 | tf_op jit(solution)/shard_map/ppermute | solution.py:401
  111.3 8.4 %collective-permute-start.10 = (bf16[128,256]{1,0:T(8,128)(2,1)S(1)}, bf16[128,256]{1,0:T(8,128)(2,1)S(1)}, u32[]{:S(2)}, u32[]{:S(2)}) collective-permute-start(bf16[128,256]{1,0:T(8,128)(2,1)S(1)} %merge.1.v0), channel_id=1, source_target_pairs={{3,0},{0,1},{1,2},{2,3},{7,4},{4,5},{5,6},{6,7},{11,8},{8,9},{9,10... | collective-permute-start | bytes 196616 | tf_op jit(solution)/shard_map/ppermute | solution.py:397
  115.3 8.6 %collective-permute-start.9 = (bf16[128,256]{1,0:T(8,128)(2,1)S(1)}, bf16[128,256]{1,0:T(8,128)(2,1)S(1)}, u32[]{:S(2)}, u32[]{:S(2)}) collective-permute-start(bf16[128,256]{1,0:T(8,128)(2,1)S(1)} %merge.1.v0), channel_id=1, source_target_pairs={{2,0},{3,1},{0,2},{1,3},{6,4},{7,5},{4,6},{5,7},{10,8},{11,9},{8,1... | collective-permute-start | bytes 196616 | tf_op jit(solution)/shard_map/ppermute | solution.py:397
  116.4 7.5 %collective-permute-start.8 = (bf16[128,256]{1,0:T(8,128)(2,1)S(1)}, bf16[128,256]{1,0:T(8,128)(2,1)S(1)}, u32[]{:S(2)}, u32[]{:S(2)}) collective-permute-start(bf16[128,256]{1,0:T(8,128)(2,1)S(1)} %merge.1.v0), channel_id=1, source_target_pairs={{1,0},{2,1},{3,2},{0,3},{5,4},{6,5},{7,6},{4,7},{9,8},{10,9},{11,1... | collective-permute-start | bytes 196616 | tf_op jit(solution)/shard_map/ppermute | solution.py:397
  118.9 0.7 copy-start.1
  126.7 2.0 copy-start.3
  128.7 8.8 %copy-start.30 = (bf16[1,2048,352]{1,2,0:T(8,128)(2,1)S(1)}, bf16[1,2048,352]{1,2,0:T(8,128)(2,1)}, u32[]{:S(2)}) copy-start(bf16[1,2048,352]{1,2,0:T(8,128)(2,1)} %param.30) | copy-start | bytes 4325380
  128.7 62.9 %all-to-all-start.2 = ((bf16[64,16,2048]{2,1,0:T(8,128)(2,1)}), bf16[64,16,2048]{2,1,0:T(8,128)(2,1)}, u32[]{:S(2)}, u32[]{:S(2)}) async-start(bf16[64,16,2048]{2,1,0:T(8,128)(2,1)} %bitcast.24), calls=%async_computation.2 | async-start | bytes 8388608 | tf_op jit(solution)/shard_map/all_to_all | solution.py:418
  137.5 1.6 copy-start.31
  191.6 1.4 copy-start.8
  202.8 2.0 copy-start
  204.8 60.1 %copy-start.2 = (bf16[128,1024]{1,0:T(8,128)(2,1)S(1)}, bf16[128,1024]{1,0:T(8,128)(2,1)}, u32[]{:S(2)}) copy-start(bf16[128,1024]{1,0:T(8,128)(2,1)} %copy-done.1) | copy-start | bytes 786436
  204.8 60.1 %all-to-all-start.3 = ((bf16[64,16,2048]{2,1,0:T(8,128)(2,1)}), bf16[64,16,2048]{2,1,0:T(8,128)(2,1)}, u32[]{:S(2)}, u32[]{:S(2)}) async-start(bf16[64,16,2048]{2,1,0:T(8,128)(2,1)} %bitcast.23), calls=%async_computation.3 | async-start | bytes 8388608 | tf_op jit(solution)/shard_map/all_to_all | solution.py:431
  270.0 9.9 %collective-permute-start.18 = (bf16[128,512]{1,0:T(8,128)(2,1)S(1)}, bf16[128,512]{1,0:T(8,128)(2,1)S(1)}, u32[]{:S(2)}, u32[]{:S(2)}) collective-permute-start(bf16[128,512]{1,0:T(8,128)(2,1)S(1)} %combine.5), channel_id=1, source_target_pairs={{3,0},{0,1},{1,2},{2,3},{7,4},{4,5},{5,6},{6,7},{11,8},{8,9},{9,10... | collective-permute-start | bytes 393224 | tf_op jit(solution)/shard_map/ppermute | solution.py:454
  272.5 11.0 %collective-permute-start.19 = (bf16[128,512]{1,0:T(8,128)(2,1)S(1)}, bf16[128,512]{1,0:T(8,128)(2,1)S(1)}, u32[]{:S(2)}, u32[]{:S(2)}) collective-permute-start(bf16[128,512]{1,0:T(8,128)(2,1)S(1)} %combine.6), channel_id=1, source_target_pairs={{2,0},{3,1},{0,2},{1,3},{6,4},{7,5},{4,6},{5,7},{10,8},{11,9},{8,1... | collective-permute-start | bytes 393224 | tf_op jit(solution)/shard_map/ppermute | solution.py:454
  274.1 13.1 %collective-permute-start.20 = (bf16[128,512]{1,0:T(8,128)(2,1)S(1)}, bf16[128,512]{1,0:T(8,128)(2,1)S(1)}, u32[]{:S(2)}, u32[]{:S(2)}) collective-permute-start(bf16[128,512]{1,0:T(8,128)(2,1)S(1)} %combine.7), channel_id=1, source_target_pairs={{1,0},{2,1},{3,2},{0,3},{5,4},{6,5},{7,6},{4,7},{9,8},{10,9},{11,1... | collective-permute-start | bytes 393224 | tf_op jit(solution)/shard_map/ppermute | solution.py:454

commit v3 on v2

--- a/solution.py
+++ b/solution.py
@@ -310,7 +310,10 @@
     quarter = d // tensor_count
     prefix = page_table.shape[1] * page_pool.shape[1]
     tok = token_order.reshape(seq_count, n)
-    params = pltpu.CompilerParams(vmem_limit_bytes=28 << 20)
+    params = pltpu.CompilerParams(vmem_limit_bytes=56 << 20)
+    large = pltpu.CompilerParams(vmem_limit_bytes=56 << 20)
+    attend_params = pltpu.CompilerParams(vmem_limit_bytes=56 << 20)
+    expert_params = pltpu.CompilerParams(vmem_limit_bytes=28 << 20)
 
     m = NZ * NY
 
@@ -330,7 +333,7 @@
         ),
         in_specs=[pl.BlockSpec(memory_space=SM)] + whole(8),
         out_specs=tuple(whole(2)),
-        compiler_params=params,
+        compiler_params=large,
         name="project",
     )(
         suffix_lengths, tok, jnp.asarray(freq[:, None], F32), jnp.asarray(np.tile(freq, 4)[None, :], F32), hidden,
@@ -378,7 +381,7 @@
                 pltpu.SMEM((seq_count,), jnp.int32),
             ],
         ),
-        compiler_params=params,
+        compiler_params=attend_params,
         name="attend",
     )(
         suffix_lengths, request_group, page_table, tok, queries, pages_a, pages_b, lat_a, lat_b, w_key_up, w_value_up
@@ -405,7 +408,7 @@
     block = rows // 4
     outbound, mixed = pl.pallas_call(
         dispatch_kernel,
-        out_shape=(jax.ShapeDtypeStruct((rows, d), BF), piece),
+        out_shape=(pltpu.HBM((rows, d), BF), piece),
         grid=(rows // block,),
         in_specs=[fixed(values.shape)] * 4
         + [fixed(hidden.shape), fixed(w_out.shape), fixed(wide.shape), fixed(wide.shape), fixed((1, d))]
@@ -421,11 +424,11 @@
     both = jnp.concatenate([w_gate_exp[0], fill, w_up_exp[0], fill], axis=1)
     results = pl.pallas_call(
         expert_kernel,
-        out_shape=jax.ShapeDtypeStruct((rows, d), BF),
+        out_shape=pltpu.HBM((rows, d), BF),
         grid=(rows // block,),
         in_specs=[pl.BlockSpec((block, d), lambda i: (i, 0)), fixed(both.shape), fixed((hid, d))],
         out_specs=pl.BlockSpec((block, d), lambda i: (i, 0)),
-        compiler_params=params,
+        compiler_params=expert_params,
         name="expert",
     )(arrived.reshape(rows, d), both, w_down_exp[0])
     back = lax.all_to_all(results.reshape(seq_count, SLOTS, d), "seq", 0, 0, tiled=True)
@@ -454,7 +457,7 @@
         sums[i] = lax.ppermute(combined(i), "tensor", tensor_from(-i, tensor_count))
     sums[0] = combined(0)
     hidden_out = pl.pallas_call(
-        finish_kernel, out_shape=piece, in_specs=whole(5), out_specs=whole(1)[0], compiler_params=params, name="finish"
+        finish_kernel, out_shape=piece, in_specs=whole(5), out_specs=whole(1)[0], compiler_params=expert_params, name="finish"
     )(mixed, *sums)
     width = KEY // tensor_count
     cache_part = lax.dynamic_slice_in_dim(latent, tensor_index * width, width, 0).T

time: 289 us -> 287 us (level)
  Pallas kernels: 43.9 us -> 59.6 us
  local copies, waits for them, and re-layouts: 24.8 us -> 11 us
  waiting for transfers between devices: 145 us -> 141 us
    unnamed x74 -> x50, local copies, waits for them, and re-layouts: 23.3 us -> 9.3 us
    pallas_call x2, Pallas kernels: 12.7 us -> 17.9 us  [the longest x1 10.9 us: local(): pl.pallas_call(expert_kernel, out_shape=pltpu.HBM((rows, d), BF), grid=(r...]
    pallas_call x4, Pallas kernels: 6.68 us -> 9.96 us  [combined(): pl.pallas_call(combine_kernel, out_shape=piece, grid_spec=pltpu.PrefetchS...]
  transfers between devices with their start and end apart: 25 -> 25, of which waited for: 13 -> 13; matrix products, arithmetic and copies ran while one was open for 3% -> 3% of each run, Pallas kernels for 1% -> 3%
where the time goes in v3:
time: 287 us; the launch traced here: 286 us
  waiting for transfers between devices  141 us (49%)
  starting transfers between devices  69.7 us (24%)
  Pallas kernels  59.6 us (21%)
  local copies, waits for them, and re-layouts  11 us (4%)
  other arithmetic  3.46 us (1%)
    all_to_all x1, waiting for transfers between devices, local(): lax.all_to_all(results.reshape(seq_count, SLOTS, d), 'seq', 0, 0, tiled=T...  54.1 us
    all_to_all x1, waiting for transfers between devices, local(): lax.all_to_all(outbound.reshape(seq_count, SLOTS, d), 'seq', 0, 0, tiled=...  47.5 us
    pallas_call x1, Pallas kernels, local(): pl.pallas_call(attend_kernel, out_shape=jax.ShapeDtypeStruct((m, n + STAT...  21.7 us
    ppermute x3, waiting for transfers between devices, local(): lax.ppermute(other, 'seq', seq_perm(i, 0, 0, 0))  12.2 us
    pallas_call x1, Pallas kernels, local(): pl.pallas_call(expert_kernel, out_shape=pltpu.HBM((rows, d), BF), grid=(r...  10.9 us
    ppermute x3, waiting for transfers between devices, local(): lax.ppermute(mine, 'tensor', tensor_from(j, tensor_count))  10.8 us
    pallas_call x4, Pallas kernels, combined(): pl.pallas_call(combine_kernel, out_shape=piece, grid_spec=pltpu.PrefetchS...  9.96 us
    ppermute x3, starting transfers between devices, local(): lax.ppermute(mine, 'tensor', tensor_from(j, tensor_count))  9.67 us
  transfers between devices with their start and end apart: 25, of which 13 were waited for; matrix products, arithmetic and copies ran while one was open for 3% of the time, Pallas kernels for 3%

profile of v3, /device:TPU:1, one launch (start us, length us, event | category | flops | bytes accessed | tf_op | source)
XLA Modules:
  0.0 286.0 jit_solution(12830700817898975276)
XLA Ops:
  0.6 4.4 %project.1 = (bf16[8,128,384]{2,1,0:T(8,128)(2,1)}, bf16[576,128]{1,0:T(8,128)(2,1)}) custom-call(s32[16]{0:T(128)} %lengths.3, s32[64,128]{1,0:T(8,128)} %bitcast.33, f32[32,1]{1,0:T(8,128)} %constant.34.clone.fcol_ref, f32[1,128]{1,0:T(1,128)} %constant.35.clone.frow_ref, bf16[128,2048]{1,0:T(8,128)(2,1)} %hid_ref.3, f32[1,2048]{1,0:T(1,128)} %bitcast.38, ...), custom_call_target="tpu_custom_call" | custom-call | tf_op jit(solution)/shard_map/project/pallas_call | solution.py:328
  5.1 6.5 %all-to-all-start = ((bf16[8,128,384]{2,1,0:T(8,128)(2,1)}), bf16[8,128,384]{2,1,0:T(8,128)(2,1)S(1)}, u32[]{:S(2)}, u32[]{:S(2)}) async-start(bf16[8,128,384]{2,1,0:T(8,128)(2,1)} %get-tuple-element.13), calls=%async_computation | async-start | bytes 1572864 | tf_op jit(solution)/shard_map/all_to_all | solution.py:344
  11.6 1.3 collective-permute-start.2
  12.9 2.4 collective-permute-start.1
  15.3 1.2 collective-permute-start
  16.5 0.3 collective-permute-start.6
  16.8 2.4 collective-permute-start.4
  19.2 0.1 collective-permute-start.5
  19.3 2.2 collective-permute-done.1
  21.5 0.1 pad_maximum_fusion.1.pa_ref
  21.5 3.3 %collective-permute-start.3 = (bf16[576,512]{1,0:T(8,128)(2,1)S(1)}, bf16[576,512]{1,0:T(8,128)(2,1)S(1)}, u32[]{:S(2)}, u32[]{:S(2)}) collective-permute-start(bf16[576,512]{1,0:T(8,128)(2,1)S(1)} %pad_maximum_fusion.1.pa_ref), channel_id=1, source_target_pairs={{4,0},{0,4},{12,8},{8,12},{20,16},{16,20},{28,24},{24,28},{36,32},... | collective-permute-start | bytes 1769480 | tf_op jit(solution)/shard_map/ppermute | solution.py:323
  24.9 2.9 %collective-permute-done.5 = bf16[576,128]{1,0:T(8,128)(2,1)S(1)} collective-permute-done((bf16[576,128]{1,0:T(8,128)(2,1)S(1)}, bf16[576,128]{1,0:T(8,128)(2,1)S(1)}, u32[]{:S(2)}, u32[]{:S(2)}) %collective-permute-start.5) | collective-permute-done | bytes 147488 | tf_op jit(solution)/shard_map/ppermute | solution.py:321
  27.9 1.9 collective-permute-start.7
  29.8 1.6 collective-permute-done.7.lb_ref
  31.4 0.8 copy-done.12
  32.2 0.9 copy-done.3
  33.1 21.7 %attend.1 = bf16[8,144,256]{2,1,0:T(8,128)(2,1)} custom-call(s32[16]{0:T(128)} %lengths.3, s32[16]{0:T(128)} %group.1, s32[4,16]{1,0:T(4,128)} %table.1, s32[64,128]{1,0:T(8,128)} %bitcast.34, bf16[8,128,384]{2,1,0:T(8,128)(2,1)} %copy-done.3, bf16[576,512]{1,0:T(8,128)(2,1)} %copy-done.5, bf16[576,512]{1,0:T(8,128)(2,1)} %copy-done.11, ...), custom_call_target="tpu_custom_call" | custom-call | tf_op jit(solution)/shard_map/attend/pallas_call | solution.py:367
  54.8 5.1 %all-to-all-start.1 = ((bf16[8,144,256]{2,1,0:T(8,128)(2,1)}), bf16[8,144,256]{2,1,0:T(8,128)(2,1)S(1)}, u32[]{:S(2)}, u32[]{:S(2)}) async-start(bf16[8,144,256]{2,1,0:T(8,128)(2,1)} %attend.1), calls=%async_computation.1 | async-start | bytes 1179648 | tf_op jit(solution)/shard_map/all_to_all | solution.py:390
  59.9 0.9 constant_dynamic-slice_fusion
  60.8 3.1 %collective-permute-start.13 = (bf16[256,256]{1,0:T(8,128)(2,1)S(1)}, bf16[256,256]{1,0:T(8,128)(2,1)S(1)}, u32[]{:S(2)}, u32[]{:S(2)}) collective-permute-start(bf16[256,256]{1,0:T(8,128)(2,1)S(1)} %constant_dynamic-slice_fusion), channel_id=1, source_target_pairs={{3,0},{0,1},{1,2},{2,3},{7,4},{4,5},{5,6},{6,7},{11,8},{8,9},{9,10... | collective-permute-start | bytes 393224 | tf_op jit(solution)/shard_map/ppermute | solution.py:349
  63.9 4.2 %collective-permute-start.12 = (bf16[256,256]{1,0:T(8,128)(2,1)S(1)}, bf16[256,256]{1,0:T(8,128)(2,1)S(1)}, u32[]{:S(2)}, u32[]{:S(2)}) collective-permute-start(bf16[256,256]{1,0:T(8,128)(2,1)S(1)} %constant_dynamic-slice_fusion), channel_id=1, source_target_pairs={{2,0},{3,1},{0,2},{1,3},{6,4},{7,5},{4,6},{5,7},{10,8},{11,9},{8,1... | collective-permute-start | bytes 393224 | tf_op jit(solution)/shard_map/ppermute | solution.py:349
  68.1 2.4 collective-permute-start.11
  70.5 7.1 %collective-permute-done.13 = bf16[256,256]{1,0:T(8,128)(2,1)S(1)} collective-permute-done((bf16[256,256]{1,0:T(8,128)(2,1)S(1)}, bf16[256,256]{1,0:T(8,128)(2,1)S(1)}, u32[]{:S(2)}, u32[]{:S(2)}) %collective-permute-start.13) | collective-permute-done | bytes 131104 | tf_op jit(solution)/shard_map/ppermute | solution.py:349
  77.6 3.7 %collective-permute-done.12 = bf16[256,256]{1,0:T(8,128)(2,1)S(1)} collective-permute-done((bf16[256,256]{1,0:T(8,128)(2,1)S(1)}, bf16[256,256]{1,0:T(8,128)(2,1)S(1)}, u32[]{:S(2)}, u32[]{:S(2)}) %collective-permute-start.12) | collective-permute-done | bytes 131104 | tf_op jit(solution)/shard_map/ppermute | solution.py:349
  81.3 2.1 collective-permute-start.16
  83.4 1.7 collective-permute-start.15
  85.1 0.8 collective-permute-start.14
  85.9 0.8 copy-done.6
  86.7 2.9 %merge.1.v0 = bf16[128,256]{1,0:T(8,128)(2,1)} custom-call(bf16[8,144,256]{2,1,0:T(8,128)(2,1)} %copy-done.6), custom_call_target="tpu_custom_call" | custom-call | tf_op jit(solution)/shard_map/merge/pallas_call | solution.py:391
  89.6 1.7 collective-permute-done.16
  91.3 9.2 %collective-permute-done.15 = bf16[3,256,256]{2,1,0:T(8,128)(2,1)S(1)} collective-permute-done((bf16[3,256,256]{2,1,0:T(8,128)(2,1)S(1)}, bf16[3,256,256]{2,1,0:T(8,128)(2,1)S(1)}, u32[]{:S(2)}, u32[]{:S(2)}) %collective-permute-start.15) | collective-permute-done | bytes 393248 | tf_op jit(solution)/shard_map/ppermute | solution.py:350
  100.6 1.2 collective-permute-done.14
  102.0 1.8 collective-permute-start.17
  103.8 4.0 %collective-permute-start.10 = (bf16[128,256]{1,0:T(8,128)(2,1)S(1)}, bf16[128,256]{1,0:T(8,128)(2,1)S(1)}, u32[]{:S(2)}, u32[]{:S(2)}) collective-permute-start(bf16[128,256]{1,0:T(8,128)(2,1)S(1)} %copy-done.13), channel_id=1, source_target_pairs={{3,0},{0,1},{1,2},{2,3},{7,4},{4,5},{5,6},{6,7},{11,8},{8,9},{9,10... | collective-permute-start | bytes 196616 | tf_op jit(solution)/shard_map/ppermute | solution.py:400
  107.8 1.1 collective-permute-start.9
  108.9 2.1 collective-permute-start.8
  111.1 1.9 slots.1
  113.0 3.2 %collective-permute-done.9.v2 = bf16[128,256]{1,0:T(8,128)(2,1)S(1)} collective-permute-done((bf16[128,256]{1,0:T(8,128)(2,1)S(1)}, bf16[128,256]{1,0:T(8,128)(2,1)S(1)}, u32[]{:S(2)}, u32[]{:S(2)}) %collective-permute-start.9) | collective-permute-done | bytes 65568 | tf_op jit(solution)/shard_map/ppermute | solution.py:400
  116.3 0.6 copy-done.19
  116.9 0.0 copy-done.20
  116.9 0.5 copy-done.7
  117.4 7.1 %dispatch.1 = (bf16[1024,2048]{1,0:T(8,128)(2,1)}, bf16[128,512]{1,0:T(8,128)(2,1)}) custom-call(bf16[128,256]{1,0:T(8,128)(2,1)} %merge.1.v0, bf16[128,256]{1,0:T(8,128)(2,1)} %copy-done.20, bf16[128,256]{1,0:T(8,128)(2,1)} %copy-done.19, bf16[128,256]{1,0:T(8,128)(2,1)} %copy-done.18, bf16[128,2048]{1,0:T(8,128)(2,1)} %hid_ref.3, ...), custom_call_target="tpu_custom_call" | custom-call | tf_op jit(solution)/shard_map/dispatch/pallas_call | solution.py:409
  124.5 8.9 %all-to-all-start.2 = ((bf16[64,16,2048]{2,1,0:T(8,128)(2,1)}), bf16[64,16,2048]{2,1,0:T(8,128)(2,1)}, u32[]{:S(2)}, u32[]{:S(2)}) async-start(bf16[64,16,2048]{2,1,0:T(8,128)(2,1)} %bitcast.27), calls=%async_computation.2 | async-start | bytes 8388608 | tf_op jit(solution)/shard_map/all_to_all | solution.py:421
  133.4 1.6 copy.23
  135.0 1.6 copy.24
  136.6 0.1 broadcast_in_dim.3
  136.6 3.3 %pad_maximum_fusion.wgu_ref = bf16[2048,768]{1,0:T(8,128)(2,1)S(1)} fusion(bf16[2048,32]{1,0:T(8,128)(2,1)S(1)} %broadcast_in_dim.3, bf16[2048,352]{1,0:T(8,128)(2,1)} %bitcast.26, bf16[2048,352]{1,0:T(8,128)(2,1)} %bitcast.25), kind=kLoop, calls=%fused_computation | loop fusion | flops 12582912 | bytes 6160384 | tf_op jit(solution)/shard_map/concatenate | solution.py:424
  140.0 47.5 %all-to-all-done.2 = bf16[64,16,2048]{2,1,0:T(8,128)(2,1)} async-done(((bf16[64,16,2048]{2,1,0:T(8,128)(2,1)}), bf16[64,16,2048]{2,1,0:T(8,128)(2,1)}, u32[]{:S(2)}, u32[]{:S(2)}) %all-to-all-start.2) | async-done | bytes 4194336 | tf_op jit(solution)/shard_map/all_to_all | solution.py:421
  187.5 1.4 copy-done
  188.9 10.9 %expert.1 = bf16[1024,2048]{1,0:T(8,128)(2,1)} custom-call(bf16[1024,2048]{1,0:T(8,128)(2,1)} %bitcast.15.x_ref, bf16[2048,768]{1,0:T(8,128)(2,1)S(1)} %pad_maximum_fusion.wgu_ref, bf16[352,2048]{1,0:T(8,128)(2,1)S(1)} %bitcast.23), custom_call_target="tpu_custom_call" | custom-call | tf_op jit(solution)/shard_map/expert/pallas_call | solution.py:425
  199.7 5.9 %all-to-all-start.3 = ((bf16[64,16,2048]{2,1,0:T(8,128)(2,1)}), bf16[64,16,2048]{2,1,0:T(8,128)(2,1)}, u32[]{:S(2)}, u32[]{:S(2)}) async-start(bf16[64,16,2048]{2,1,0:T(8,128)(2,1)} %bitcast.24), calls=%async_computation.3 | async-start | bytes 8388608 | tf_op jit(solution)/shard_map/all_to_all | solution.py:434
  205.7 54.1 %all-to-all-done.3 = bf16[64,16,2048]{2,1,0:T(8,128)(2,1)} async-done(((bf16[64,16,2048]{2,1,0:T(8,128)(2,1)}), bf16[64,16,2048]{2,1,0:T(8,128)(2,1)}, u32[]{:S(2)}, u32[]{:S(2)}) %all-to-all-start.3) | async-done | bytes 4194336 | tf_op jit(solution)/shard_map/all_to_all | solution.py:434
  259.7 2.5 combine.7
  262.2 2.5 combine.6
  264.7 2.5 combine.5
  267.2 2.3 collective-permute-start.18
  269.5 1.5 collective-permute-start.19
  270.9 3.3 %collective-permute-start.20 = (bf16[128,512]{1,0:T(8,128)(2,1)S(1)}, bf16[128,512]{1,0:T(8,128)(2,1)S(1)}, u32[]{:S(2)}, u32[]{:S(2)}) collective-permute-start(bf16[128,512]{1,0:T(8,128)(2,1)S(1)} %copy-done.16), channel_id=1, source_target_pairs={{1,0},{2,1},{3,2},{0,3},{5,4},{6,5},{7,6},{4,7},{9,8},{10,9},{11,1... | collective-permute-start | bytes 393224 | tf_op jit(solution)/shard_map/ppermute | solution.py:457
  274.2 0.6 dynamic-slice_bitcast_fusion
  274.9 2.5 combine.4.a_ref
  277.4 2.3 collective-permute-done.19.c_ref
  279.7 4.7 %collective-permute-done.20.d_ref = bf16[128,512]{1,0:T(8,128)(2,1)S(1)} collective-permute-done((bf16[128,512]{1,0:T(8,128)(2,1)S(1)}, bf16[128,512]{1,0:T(8,128)(2,1)S(1)}, u32[]{:S(2)}, u32[]{:S(2)}) %collective-permute-start.20) | collective-permute-done | bytes 131104 | tf_op jit(solution)/shard_map/ppermute | solution.py:457
  284.4 0.9 copy-done.1
  285.3 0.7 finish.1
  (55 shorter events, 0.4 us)
Async XLA Ops:
  5.1 6.5 %copy-start.15 = (bf16[1,128,576]{1,2,0:T(8,128)(2,1)S(1)}, bf16[1,128,576]{1,2,0:T(8,128)(2,1)}, u32[]{:S(2)}) copy-start(bf16[1,128,576]{1,2,0:T(8,128)(2,1)} %param.33) | copy-start | bytes 442372
  5.1 11.4 %copy-start.14 = (bf16[576,128]{1,0:T(8,128)(2,1)S(1)}, bf16[576,128]{1,0:T(8,128)(2,1)}, u32[]{:S(2)}) copy-start(bf16[576,128]{1,0:T(8,128)(2,1)} %get-tuple-element.14) | copy-start | bytes 442372
  5.1 26.4 %all-to-all-start = ((bf16[8,128,384]{2,1,0:T(8,128)(2,1)}), bf16[8,128,384]{2,1,0:T(8,128)(2,1)S(1)}, u32[]{:S(2)}, u32[]{:S(2)}) async-start(bf16[8,128,384]{2,1,0:T(8,128)(2,1)} %get-tuple-element.13), calls=%async_computation | async-start | bytes 1572864 | tf_op jit(solution)/shard_map/all_to_all | solution.py:344
  11.6 7.6 %collective-permute-start.2 = (bf16[576,128]{1,0:T(8,128)(2,1)S(1)}, bf16[576,128]{1,0:T(8,128)(2,1)S(1)}, u32[]{:S(2)}, u32[]{:S(2)}) collective-permute-start(bf16[576,128]{1,0:T(8,128)(2,1)S(1)} %bitcast.29), channel_id=1, source_target_pairs={{192,0},{196,4},{200,8},{204,12},{208,16},{212,20},{216,24},{220,2... | collective-permute-start | bytes 442376 | tf_op jit(solution)/shard_map/ppermute | solution.py:321
  12.9 8.6 %collective-permute-start.1 = (bf16[576,128]{1,0:T(8,128)(2,1)S(1)}, bf16[576,128]{1,0:T(8,128)(2,1)S(1)}, u32[]{:S(2)}, u32[]{:S(2)}) collective-permute-start(bf16[576,128]{1,0:T(8,128)(2,1)S(1)} %bitcast.30), channel_id=1, source_target_pairs={{128,0},{132,4},{136,8},{140,12},{144,16},{148,20},{152,24},{156,2... | collective-permute-start | bytes 442376 | tf_op jit(solution)/shard_map/ppermute | solution.py:321
  15.3 6.1 %collective-permute-start = (bf16[576,128]{1,0:T(8,128)(2,1)S(1)}, bf16[576,128]{1,0:T(8,128)(2,1)S(1)}, u32[]{:S(2)}, u32[]{:S(2)}) collective-permute-start(bf16[576,128]{1,0:T(8,128)(2,1)S(1)} %bitcast.31), channel_id=1, source_target_pairs={{64,0},{68,4},{72,8},{76,12},{80,16},{84,20},{88,24},{92,28},{96,3... | collective-permute-start | bytes 442376 | tf_op jit(solution)/shard_map/ppermute | solution.py:321
  16.5 11.3 %collective-permute-start.6 = (bf16[576,128]{1,0:T(8,128)(2,1)S(1)}, bf16[576,128]{1,0:T(8,128)(2,1)S(1)}, u32[]{:S(2)}, u32[]{:S(2)}) collective-permute-start(bf16[576,128]{1,0:T(8,128)(2,1)S(1)} %copy-done.14), channel_id=1, source_target_pairs={{192,0},{196,4},{200,8},{204,12},{208,16},{212,20},{216,24},{220,2... | collective-permute-start | bytes 442376 | tf_op jit(solution)/shard_map/ppermute | solution.py:321
  16.8 8.1 %collective-permute-start.4 = (bf16[576,128]{1,0:T(8,128)(2,1)S(1)}, bf16[576,128]{1,0:T(8,128)(2,1)S(1)}, u32[]{:S(2)}, u32[]{:S(2)}) collective-permute-start(bf16[576,128]{1,0:T(8,128)(2,1)S(1)} %copy-done.14), channel_id=1, source_target_pairs={{64,0},{68,4},{72,8},{76,12},{80,16},{84,20},{88,24},{92,28},{96,3... | collective-permute-start | bytes 442376 | tf_op jit(solution)/shard_map/ppermute | solution.py:321
  19.2 8.6 %collective-permute-start.5 = (bf16[576,128]{1,0:T(8,128)(2,1)S(1)}, bf16[576,128]{1,0:T(8,128)(2,1)S(1)}, u32[]{:S(2)}, u32[]{:S(2)}) collective-permute-start(bf16[576,128]{1,0:T(8,128)(2,1)S(1)} %copy-done.14), channel_id=1, source_target_pairs={{128,0},{132,4},{136,8},{140,12},{144,16},{148,20},{152,24},{156,2... | collective-permute-start | bytes 442376 | tf_op jit(solution)/shard_map/ppermute | solution.py:321
  21.5 9.9 %copy-start.5 = (bf16[576,512]{1,0:T(8,128)(2,1)}, bf16[576,512]{1,0:T(8,128)(2,1)S(1)}, u32[]{:S(2)}) copy-start(bf16[576,512]{1,0:T(8,128)(2,1)S(1)} %pad_maximum_fusion.1.pa_ref) | copy-start | bytes 1769476
  21.5 8.2 %collective-permute-start.3 = (bf16[576,512]{1,0:T(8,128)(2,1)S(1)}, bf16[576,512]{1,0:T(8,128)(2,1)S(1)}, u32[]{:S(2)}, u32[]{:S(2)}) collective-permute-start(bf16[576,512]{1,0:T(8,128)(2,1)S(1)} %pad_maximum_fusion.1.pa_ref), channel_id=1, source_target_pairs={{4,0},{0,4},{12,8},{8,12},{20,16},{16,20},{28,24},{24,28},{36,32},... | collective-permute-start | bytes 1769480 | tf_op jit(solution)/shard_map/ppermute | solution.py:323
  27.9 3.6 %copy-start.10 = (bf16[576,512]{1,0:T(8,128)(2,1)}, bf16[576,512]{1,0:T(8,128)(2,1)S(1)}, u32[]{:S(2)}) copy-start(bf16[576,512]{1,0:T(8,128)(2,1)S(1)} %constant_dynamic-update-slice_fusion.la_ref) | copy-start | bytes 1769476
  27.9 3.5 %collective-permute-start.7 = (bf16[576,512]{1,0:T(8,128)(2,1)S(1)}, bf16[576,512]{1,0:T(8,128)(2,1)S(1)}, u32[]{:S(2)}, u32[]{:S(2)}) collective-permute-start(bf16[576,512]{1,0:T(8,128)(2,1)S(1)} %constant_dynamic-update-slice_fusion.la_ref), channel_id=1, source_target_pairs={{4,0},{0,4},{12,8},{8,12},{20,16},{16,20},{28,24},{24,28},{36,32},... | collective-permute-start | bytes 1769480 | tf_op jit(solution)/shard_map/ppermute | solution.py:323
  29.8 1.6 copy-start.11
  31.4 0.8 copy-start.12
  32.2 0.9 copy-start.3
  54.8 31.1 %all-to-all-start.1 = ((bf16[8,144,256]{2,1,0:T(8,128)(2,1)}), bf16[8,144,256]{2,1,0:T(8,128)(2,1)S(1)}, u32[]{:S(2)}, u32[]{:S(2)}) async-start(bf16[8,144,256]{2,1,0:T(8,128)(2,1)} %attend.1), calls=%async_computation.1 | async-start | bytes 1179648 | tf_op jit(solution)/shard_map/all_to_all | solution.py:390
  60.8 16.7 %collective-permute-start.13 = (bf16[256,256]{1,0:T(8,128)(2,1)S(1)}, bf16[256,256]{1,0:T(8,128)(2,1)S(1)}, u32[]{:S(2)}, u32[]{:S(2)}) collective-permute-start(bf16[256,256]{1,0:T(8,128)(2,1)S(1)} %constant_dynamic-slice_fusion), channel_id=1, source_target_pairs={{3,0},{0,1},{1,2},{2,3},{7,4},{4,5},{5,6},{6,7},{11,8},{8,9},{9,10... | collective-permute-start | bytes 393224 | tf_op jit(solution)/shard_map/ppermute | solution.py:349
  63.9 17.4 %collective-permute-start.12 = (bf16[256,256]{1,0:T(8,128)(2,1)S(1)}, bf16[256,256]{1,0:T(8,128)(2,1)S(1)}, u32[]{:S(2)}, u32[]{:S(2)}) collective-permute-start(bf16[256,256]{1,0:T(8,128)(2,1)S(1)} %constant_dynamic-slice_fusion), channel_id=1, source_target_pairs={{2,0},{3,1},{0,2},{1,3},{6,4},{7,5},{4,6},{5,7},{10,8},{11,9},{8,1... | collective-permute-start | bytes 393224 | tf_op jit(solution)/shard_map/ppermute | solution.py:349
  68.1 13.2 %collective-permute-start.11 = (bf16[256,256]{1,0:T(8,128)(2,1)S(1)}, bf16[256,256]{1,0:T(8,128)(2,1)S(1)}, u32[]{:S(2)}, u32[]{:S(2)}) collective-permute-start(bf16[256,256]{1,0:T(8,128)(2,1)S(1)} %constant_dynamic-slice_fusion), channel_id=1, source_target_pairs={{1,0},{2,1},{3,2},{0,3},{5,4},{6,5},{7,6},{4,7},{9,8},{10,9},{11,1... | collective-permute-start | bytes 393224 | tf_op jit(solution)/shard_map/ppermute | solution.py:349
  81.3 10.0 %collective-permute-start.16 = (bf16[3,256,256]{2,1,0:T(8,128)(2,1)S(1)}, bf16[3,256,256]{2,1,0:T(8,128)(2,1)S(1)}, u32[]{:S(2)}, u32[]{:S(2)}) collective-permute-start(bf16[3,256,256]{2,1,0:T(8,128)(2,1)S(1)} %pad_maximum_fusion.2), channel_id=1, source_target_pairs={{192,0},{196,4},{200,8},{204,12},{208,16},{212,20},{216,24},{220,2... | collective-permute-start | bytes 1179656 | tf_op jit(solution)/shard_map/ppermute | solution.py:350
  83.4 17.2 %collective-permute-start.15 = (bf16[3,256,256]{2,1,0:T(8,128)(2,1)S(1)}, bf16[3,256,256]{2,1,0:T(8,128)(2,1)S(1)}, u32[]{:S(2)}, u32[]{:S(2)}) collective-permute-start(bf16[3,256,256]{2,1,0:T(8,128)(2,1)S(1)} %pad_maximum_fusion.2), channel_id=1, source_target_pairs={{128,0},{132,4},{136,8},{140,12},{144,16},{148,20},{152,24},{156,2... | collective-permute-start | bytes 1179656 | tf_op jit(solution)/shard_map/ppermute | solution.py:350
  85.1 16.7 %collective-permute-start.14 = (bf16[3,256,256]{2,1,0:T(8,128)(2,1)S(1)}, bf16[3,256,256]{2,1,0:T(8,128)(2,1)S(1)}, u32[]{:S(2)}, u32[]{:S(2)}) collective-permute-start(bf16[3,256,256]{2,1,0:T(8,128)(2,1)S(1)} %pad_maximum_fusion.2), channel_id=1, source_target_pairs={{64,0},{68,4},{72,8},{76,12},{80,16},{84,20},{88,24},{92,28},{96,3... | collective-permute-start | bytes 1179656 | tf_op jit(solution)/shard_map/ppermute | solution.py:350
  85.9 0.8 copy-start.6
  89.6 14.2 %copy-start.13 = (bf16[128,256]{1,0:T(8,128)(2,1)S(1)}, bf16[128,256]{1,0:T(8,128)(2,1)}, u32[]{:S(2)}) copy-start(bf16[128,256]{1,0:T(8,128)(2,1)} %merge.1.v0) | copy-start | bytes 196612
  102.0 14.3 %copy-start.4 = (bf16[12,256,256]{2,1,0:T(8,128)(2,1)}, bf16[12,256,256]{2,1,0:T(8,128)(2,1)S(1)}, u32[]{:S(2)}) copy-start(bf16[12,256,256]{2,1,0:T(8,128)(2,1)S(1)} %constant_dynamic-update-slice_fusion.4.wa_ref) | copy-start | bytes 4718596
  102.0 14.3 %collective-permute-start.17 = (bf16[12,256,256]{2,1,0:T(8,128)(2,1)S(1)}, bf16[12,256,256]{2,1,0:T(8,128)(2,1)S(1)}, u32[]{:S(2)}, u32[]{:S(2)}) collective-permute-start(bf16[12,256,256]{2,1,0:T(8,128)(2,1)S(1)} %constant_dynamic-update-slice_fusion.4.wa_ref), channel_id=1, source_target_pairs={{4,0},{0,4},{12,8},{8,12},{20,16},{16,20},{28,24},{24,28},{36,32},... | collective-permute-start | bytes 4718600 | tf_op jit(solution)/shard_map/ppermute | solution.py:404
  103.8 9.2 %collective-permute-start.10 = (bf16[128,256]{1,0:T(8,128)(2,1)S(1)}, bf16[128,256]{1,0:T(8,128)(2,1)S(1)}, u32[]{:S(2)}, u32[]{:S(2)}) collective-permute-start(bf16[128,256]{1,0:T(8,128)(2,1)S(1)} %copy-done.13), channel_id=1, source_target_pairs={{3,0},{0,1},{1,2},{2,3},{7,4},{4,5},{5,6},{6,7},{11,8},{8,9},{9,10... | collective-permute-start | bytes 196616 | tf_op jit(solution)/shard_map/ppermute | solution.py:400
  107.8 8.5 %collective-permute-start.9 = (bf16[128,256]{1,0:T(8,128)(2,1)S(1)}, bf16[128,256]{1,0:T(8,128)(2,1)S(1)}, u32[]{:S(2)}, u32[]{:S(2)}) collective-permute-start(bf16[128,256]{1,0:T(8,128)(2,1)S(1)} %copy-done.13), channel_id=1, source_target_pairs={{2,0},{3,1},{0,2},{1,3},{6,4},{7,5},{4,6},{5,7},{10,8},{11,9},{8,1... | collective-permute-start | bytes 196616 | tf_op jit(solution)/shard_map/ppermute | solution.py:400
  108.9 7.3 %collective-permute-start.8 = (bf16[128,256]{1,0:T(8,128)(2,1)S(1)}, bf16[128,256]{1,0:T(8,128)(2,1)S(1)}, u32[]{:S(2)}, u32[]{:S(2)}) collective-permute-start(bf16[128,256]{1,0:T(8,128)(2,1)S(1)} %copy-done.13), channel_id=1, source_target_pairs={{1,0},{2,1},{3,2},{0,3},{5,4},{6,5},{7,6},{4,7},{9,8},{10,9},{11,1... | collective-permute-start | bytes 196616 | tf_op jit(solution)/shard_map/ppermute | solution.py:400
  113.0 3.3 %copy-start.18 = (bf16[128,256]{1,0:T(8,128)(2,1)}, bf16[128,256]{1,0:T(8,128)(2,1)S(1)}, u32[]{:S(2)}) copy-start(bf16[128,256]{1,0:T(8,128)(2,1)S(1)} %collective-permute-done.10.v3) | copy-start | bytes 196612
  116.2 0.6 copy-start.19
  116.3 0.7 copy-start.20
  116.3 1.2 copy-start.7
  124.5 8.9 %copy-start.8 = (bf16[1,2048,352]{1,2,0:T(8,128)(2,1)S(1)}, bf16[1,2048,352]{1,2,0:T(8,128)(2,1)}, u32[]{:S(2)}) copy-start(bf16[1,2048,352]{1,2,0:T(8,128)(2,1)} %param.30) | copy-start | bytes 4325380
  124.5 63.0 %all-to-all-start.2 = ((bf16[64,16,2048]{2,1,0:T(8,128)(2,1)}), bf16[64,16,2048]{2,1,0:T(8,128)(2,1)}, u32[]{:S(2)}, u32[]{:S(2)}) async-start(bf16[64,16,2048]{2,1,0:T(8,128)(2,1)} %bitcast.27), calls=%async_computation.2 | async-start | bytes 8388608 | tf_op jit(solution)/shard_map/all_to_all | solution.py:421
  133.4 1.6 copy-start.9
  187.5 1.4 copy-start
  199.7 60.0 %all-to-all-start.3 = ((bf16[64,16,2048]{2,1,0:T(8,128)(2,1)}), bf16[64,16,2048]{2,1,0:T(8,128)(2,1)}, u32[]{:S(2)}, u32[]{:S(2)}) async-start(bf16[64,16,2048]{2,1,0:T(8,128)(2,1)} %bitcast.24), calls=%async_computation.3 | async-start | bytes 8388608 | tf_op jit(solution)/shard_map/all_to_all | solution.py:434
  264.7 4.8 %copy-start.17 = (bf16[128,512]{1,0:T(8,128)(2,1)S(1)}, bf16[128,512]{1,0:T(8,128)(2,1)}, u32[]{:S(2)}) copy-start(bf16[128,512]{1,0:T(8,128)(2,1)} %combine.6) | copy-start | bytes 393220
  264.7 6.3 %copy-start.16 = (bf16[128,512]{1,0:T(8,128)(2,1)S(1)}, bf16[128,512]{1,0:T(8,128)(2,1)}, u32[]{:S(2)}) copy-start(bf16[128,512]{1,0:T(8,128)(2,1)} %combine.7) | copy-start | bytes 393220
  267.2 10.2 %collective-permute-start.18 = (bf16[128,512]{1,0:T(8,128)(2,1)}, bf16[128,512]{1,0:T(8,128)(2,1)S(1)}, u32[]{:S(2)}, u32[]{:S(2)}) collective-permute-start(bf16[128,512]{1,0:T(8,128)(2,1)} %combine.5), channel_id=1, source_target_pairs={{3,0},{0,1},{1,2},{2,3},{7,4},{4,5},{5,6},{6,7},{11,8},{8,9},{9,10... | collective-permute-start | bytes 393224 | tf_op jit(solution)/shard_map/ppermute | solution.py:457
  269.5 10.2 %collective-permute-start.19 = (bf16[128,512]{1,0:T(8,128)(2,1)S(1)}, bf16[128,512]{1,0:T(8,128)(2,1)S(1)}, u32[]{:S(2)}, u32[]{:S(2)}) collective-permute-start(bf16[128,512]{1,0:T(8,128)(2,1)S(1)} %copy-done.17), channel_id=1, source_target_pairs={{2,0},{3,1},{0,2},{1,3},{6,4},{7,5},{4,6},{5,7},{10,8},{11,9},{8,1... | collective-permute-start | bytes 393224 | tf_op jit(solution)/shard_map/ppermute | solution.py:457
  270.9 13.4 %collective-permute-start.20 = (bf16[128,512]{1,0:T(8,128)(2,1)S(1)}, bf16[128,512]{1,0:T(8,128)(2,1)S(1)}, u32[]{:S(2)}, u32[]{:S(2)}) collective-permute-start(bf16[128,512]{1,0:T(8,128)(2,1)S(1)} %copy-done.16), channel_id=1, source_target_pairs={{1,0},{2,1},{3,2},{0,3},{5,4},{6,5},{7,6},{4,7},{9,8},{10,9},{11,1... | collective-permute-start | bytes 393224 | tf_op jit(solution)/shard_map/ppermute | solution.py:457
  274.9 9.5 %copy-start.2 = (bf16[128,512]{1,0:T(8,128)(2,1)S(1)}, bf16[128,512]{1,0:T(8,128)(2,1)}, u32[]{:S(2)}) copy-start(bf16[128,512]{1,0:T(8,128)(2,1)} %get-tuple-element.20.mix_ref) | copy-start | bytes 393220
  284.4 0.9 copy-start.1
